TPU v7x, 32 devices: a whole 2x2x4 slice. The times are simulated.
32 devices in a mesh: ent: 8 (over z, x), qry: 4 (over y, core).
Axes of the slice: x: 2, y: 2, z: 4, core: 2. Of those that a mesh axis runs over, the one named last changes fastest.
Arguments:
- ent_feat: bfloat16 [64, 8192], P(None, 'ent'), may hold values from -6 to 6
- query_head: int32 [16], replicated, may hold values from 0 to 8191
- query_rel: int32 [16], replicated, may hold values from 0 to 821
- query_table: bfloat16 [822, 64], replicated, may hold values from -5 to 5
- rel_table: bfloat16 [3, 822, 64], replicated, may hold values from -5 to 5
- layer_weight: bfloat16 [3, 64, 64], replicated, may hold values from -0.75 to 0.75
- layer_bias: float32 [3, 64], replicated, may hold values from -5 to 5
- norm_gain: float32 [3, 64], replicated, may hold values from 0.5 to 1.5
- norm_shift: float32 [3, 64], replicated, may hold values from -3 to 3
- reg_blocks: int32 [640, 2], P('ent'), may hold values from 0 to 63, as said below
- reg_rel: int32 [640], P('ent'), may hold values from 0 to 821
- reg_mask: int32 [640, 128, 128], P('ent'), may hold values 0 or 1
- hin_blocks: int32 [192, 2], P('ent'), may hold values from 0 to 63, as said below
- hin_rel: int32 [192], P('ent'), may hold values from 0 to 821
- hin_mask: int32 [192, 128, 128], P('ent'), may hold values 0 or 1
- hout_blocks: int32 [192, 2], P('ent'), may hold values from 0 to 63, as said below
- hout_rel: int32 [192], P('ent'), may hold values from 0 to 821
- hout_mask: int32 [192, 128, 128], P('ent'), may hold values 0 or 1
- read_weight: bfloat16 [128, 64], replicated, may hold values from -0.5 to 0.5
- read_bias: float32 [64], replicated, may hold values from -5 to 5
- read_out: float32 [64], replicated, may hold values from -0.75 to 0.75
Outputs:
- scores: float32 [16, 8192], P(None, ('ent', 'qry'))
- hub_scores: float32 [16, 128], P('qry', 'ent')
Inputs may be any that keep to these rules, and one draw needn't show every extreme that they name: `reg_blocks`: rows are grouped by 80 per index of ent. Column 0 is a block of that index's own 8 blocks; column 1 is a block of the same index's or an adjacent index's entities. `hin_blocks`: rows are grouped by 24 per index of ent. Column 0 is a hub block, below 1; column 1 is a block of that index's own entities. `hout_blocks`: rows are grouped by 24 per index of ent. Column 0 is a block of that index's own entities; column 1 is a hub block, below 1.
All inputs are finite; a program needn't handle non-finite values. No bound on the sum of `reg_mask` or of `hin_mask` or of `hout_mask` on one device may be relied on, other than what follows from the above.
Results may differ from a plain program's by a relative error of at most 0.0075.
Values may be sent and summed in bfloat16 or wider, within the bound.
No kernel may reach another device: no remote copies, remote signals or barrier semaphores. Data moves between devices by JAX's collectives and lax.ppermute only.
A program may use at most 128 MiB of HBM per device.

v0:
```python
import jax
import jax.numpy as jnp
from jax import lax
from jax.sharding import PartitionSpec as P

LAYERS = 3
HUB_DEV = 16


def padded(cells, sides, width):
    for axis, dim in sides:
        count = lax.axis_size(axis)
        ends = count - 1
        head = lax.slice_in_dim(cells, 0, width, axis=dim)
        tail = lax.slice_in_dim(cells, cells.shape[dim] - width, cells.shape[dim], axis=dim)
        cells = jnp.concatenate(
            [
                lax.ppermute(tail, axis, [(i, (i + 1) % count) for i in range(ends)]),
                cells,
                lax.ppermute(head, axis, [((i + 1) % count, i) for i in range(ends)]),
            ],
            axis=dim,
        )
    return cells


def normalize(values, along_axis, gain_rows, shift_rows):
    average = jnp.mean(values, axis=along_axis, keepdims=True)
    centered = values - average
    variance = jnp.mean(centered * centered, axis=along_axis, keepdims=True)
    return centered * lax.rsqrt(variance + 1e-05) * gain_rows + shift_rows


def update_hubs(hub_sum, hub_old, weight, bias_row, gain_row, shift_row, q_local, model_width):
    count = hub_sum.shape[0]
    inputs_now = hub_sum.astype(jnp.bfloat16).reshape(count, q_local, model_width)
    linear = (
        jnp.einsum("hqd,de->hqe", inputs_now, weight, preferred_element_type=jnp.float32)
        + bias_row[None, None, :]
    )
    normed = normalize(linear, 2, gain_row[None, None, :], shift_row[None, None, :])
    updated = jax.nn.relu(normed) + hub_old.astype(jnp.float32).reshape(count, q_local, model_width)
    return updated.astype(jnp.bfloat16).reshape(count, q_local * model_width)


def body(
    ent_feat,
    query_head,
    query_rel,
    query_table,
    rel_table,
    layer_weight,
    layer_bias,
    norm_gain,
    norm_shift,
    reg_blocks,
    reg_rel,
    reg_mask,
    hin_blocks,
    hin_rel,
    hin_mask,
    hout_blocks,
    hout_rel,
    hout_mask,
    read_weight,
    read_bias,
    read_out,
):
    ent_devices = lax.axis_size("ent")
    queries = query_head.shape[0]
    q_local = queries // lax.axis_size("qry")
    model_width = ent_feat.shape[0]
    ent_local = ent_feat.shape[1]
    block_size = reg_mask.shape[1]
    blocks_local = ent_local // block_size
    hub_total = HUB_DEV * ent_devices
    hub_block_count = hub_total // block_size
    state_rows = q_local * model_width
    first_block = lax.axis_index("ent") * blocks_local
    first_entity = lax.axis_index("ent") * ent_local
    query_first = lax.axis_index("qry") * q_local
    highest = lax.Precision.HIGHEST
    rel_iota = jnp.arange(query_table.shape[0], dtype=jnp.int32)
    query_onehot = (query_rel[:, None] == rel_iota[None, :]).astype(jnp.bfloat16)
    query_all = jnp.dot(query_onehot, query_table, preferred_element_type=jnp.float32)
    query_local = lax.dynamic_slice_in_dim(query_all, query_first, q_local, 0)
    heads_local = lax.dynamic_slice_in_dim(query_head, query_first, q_local, 0)
    positions = first_entity + jnp.arange(ent_local, dtype=jnp.int32)
    head_hits = (heads_local[:, None] == positions[None, :]).astype(jnp.float32)
    boundary = query_local[:, :, None] * head_hits[:, None, :]
    states = (ent_feat.astype(jnp.float32)[None] + boundary).astype(jnp.bfloat16)
    reg_masks = reg_mask.astype(jnp.bfloat16)
    hin_masks = hin_mask.astype(jnp.bfloat16)
    hout_masks = hout_mask.astype(jnp.bfloat16)
    local_iota = jnp.arange(blocks_local, dtype=jnp.int32)[None, :]
    reg_onehot = (reg_blocks[:, 0][:, None] - first_block == local_iota).astype(jnp.float32)
    reg_sources = reg_blocks[:, 1] - first_block + blocks_local
    hout_onehot = (hout_blocks[:, 0][:, None] - first_block == local_iota).astype(jnp.float32)
    hout_sources = hout_blocks[:, 1]
    hin_onehot = (
        hin_blocks[:, 0][:, None] == jnp.arange(hub_block_count, dtype=jnp.int32)[None, :]
    ).astype(jnp.float32)
    hin_sources = hin_blocks[:, 1] - first_block

    def tile_coefficients(rel_ids, rel_layer):
        rel_onehot = (rel_ids[:, None] == rel_iota[None, :]).astype(jnp.bfloat16)
        rel_rows = jnp.dot(rel_onehot, rel_layer, preferred_element_type=jnp.float32)
        return (query_local[:, :, None] * rel_rows.T[None, :, :]).reshape(state_rows, -1)

    hub_own = jnp.zeros((HUB_DEV, state_rows), jnp.bfloat16)
    for layer_at in range(LAYERS):
        weight = layer_weight[layer_at]
        rel_layer = rel_table[layer_at]
        flat_states = states.reshape(state_rows, ent_local)
        window = padded(flat_states, (("ent", 1),), ent_local)
        window_blocks = window.reshape(state_rows, 3 * blocks_local, block_size)
        gathered = jnp.take(window_blocks, reg_sources, axis=1)
        product = jnp.einsum(
            "ctj,tjk->ctk", gathered, reg_masks, preferred_element_type=jnp.float32
        )
        product = product * tile_coefficients(reg_rel, rel_layer)[:, :, None]
        totals = jnp.einsum("ctk,tb->cbk", product, reg_onehot, precision=highest)
        if layer_at > 0:
            hub_full = lax.all_gather(hub_own, "ent", axis=0, tiled=True)
        else:
            hub_full = jnp.zeros((hub_total, state_rows), jnp.bfloat16)
        hub_view = hub_full.reshape(hub_block_count, block_size, state_rows)
        hub_sources = jnp.take(hub_view, hout_sources, axis=0)
        product = jnp.einsum(
            "tjc,tjk->ctk", hub_sources, hout_masks, preferred_element_type=jnp.float32
        )
        product = product * tile_coefficients(hout_rel, rel_layer)[:, :, None]
        totals = totals + jnp.einsum("ctk,tb->cbk", product, hout_onehot, precision=highest)
        own_blocks = flat_states.reshape(state_rows, blocks_local, block_size)
        hin_gathered = jnp.take(own_blocks, hin_sources, axis=1)
        hin_product = jnp.einsum(
            "ctj,tjk->tkc", hin_gathered, hin_masks, preferred_element_type=jnp.float32
        )
        hin_product = hin_product * tile_coefficients(hin_rel, rel_layer).T[:, None, :]
        partial_value = jnp.einsum(
            "tkc,th->hkc", hin_product, hin_onehot, precision=highest
        ).reshape(hub_total, state_rows)
        inputs_now = (totals.reshape(q_local, model_width, ent_local) + boundary).astype(
            jnp.bfloat16
        )
        linear = (
            jnp.einsum("qdv,de->qev", inputs_now, weight, preferred_element_type=jnp.float32)
            + layer_bias[layer_at][None, :, None]
        )
        normed = normalize(
            linear, 1, norm_gain[layer_at][None, :, None], norm_shift[layer_at][None, :, None]
        )
        states = (jax.nn.relu(normed) + states.astype(jnp.float32)).astype(jnp.bfloat16)
        hub_sum = lax.psum_scatter(partial_value, "ent", scatter_dimension=0, tiled=True)
        hub_own = update_hubs(
            hub_sum,
            hub_own,
            weight,
            layer_bias[layer_at],
            norm_gain[layer_at],
            norm_shift[layer_at],
            q_local,
            model_width,
        )
    read_states = read_weight[:model_width]
    query_part_all = (
        jnp.dot(
            query_all.astype(jnp.bfloat16),
            read_weight[model_width:],
            preferred_element_type=jnp.float32,
        )
        + read_bias[None, :]
    )
    query_part_local = lax.dynamic_slice_in_dim(query_part_all, query_first, q_local, 0)
    moved_states = lax.all_to_all(states, "qry", split_axis=2, concat_axis=0, tiled=True)
    features = jax.nn.relu(
        jnp.einsum("qdv,de->qev", moved_states, read_states, preferred_element_type=jnp.float32)
        + query_part_all[:, :, None]
    )
    scores = jnp.einsum("qev,e->qv", features, read_out, precision=highest)
    hub_view_own = hub_own.reshape(HUB_DEV, q_local, model_width)
    hub_features = jax.nn.relu(
        jnp.einsum("hqd,de->hqe", hub_view_own, read_states, preferred_element_type=jnp.float32)
        + query_part_local[None]
    )
    hub_scores = jnp.einsum("hqe,e->qh", hub_features, read_out, precision=highest)
    return (scores, hub_scores)


def solution(mesh):
    return jax.shard_map(
        body,
        mesh=mesh,
        in_specs=(
            P(None, "ent"),
            P(),
            P(),
            P(),
            P(),
            P(),
            P(),
            P(),
            P(),
            P("ent", None),
            P("ent"),
            P("ent", None, None),
            P("ent", None),
            P("ent"),
            P("ent", None, None),
            P("ent", None),
            P("ent"),
            P("ent", None, None),
            P(),
            P(),
            P(),
        ),
        out_specs=(P(None, ("ent", "qry")), P("qry", "ent")),
        check_vma=False,
    )
```

profile of v0, /device:TPU:0, one launch (start us, length us, event | category | flops | bytes accessed | tf_op | source)
XLA Modules:
  0.0 461.2 jit_solution(1653198230750983543)
XLA Ops:
  13.4 6.3 %collective-permute-start = (bf16[256,1024]{1,0:T(8,128)(2,1)}, bf16[256,1024]{1,0:T(8,128)(2,1)}, u32[]{:S(2)}, u32[]{:S(2)}) collective-permute-start(bf16[256,1024]{1,0:T(8,128)(2,1)} %fusion.90), channel_id=1, source_target_pairs={{0,4},{4,8},{8,12},{12,16},{16,20},{20,24},{24,28},{1,5},{5,9},{9,... | collective-permute-start | bytes 1572872 | tf_op jit(solution)/shard_map/ppermute | solution.py:18
  37.9 4.0 multiply_bitcast_fusion.2
  56.1 3.9 fusion.28
  64.0 48.3 %reduce-scatter.4.cloned.1.call-done = f32[16,256]{1,0:T(8,128)} async-done(((f32[128,256]{1,0:T(8,128)}), f32[16,256]{1,0:T(8,128)}) %reduce-scatter.4.cloned.1.call-update) | async-done | bytes 16400 | tf_op jit(solution)/shard_map/reduce_scatter | solution.py:154
  117.5 5.9 %gather_fusion = bf16[80,256,128]{2,1,0:T(8,128)(2,1)} fusion(bf16[256,24,128]{2,0,1:T(8,128)(2,1)S(1)} %copy.179, s32[1024]{0:T(1024)} %pad_clamp_fusion.1), kind=kCustom, calls=%fused_computation.clone | custom fusion | bytes 10486080 | tf_op jit(solution)/shard_map/jit(_take)/gather | solution.py:117
  123.5 6.6 %bitcast_multiply_fusion.2 = f32[256,80,128]{2,0,1:T(8,128)S(1)} fusion(f32[256,80]{0,1:T(8,128)S(1)} %copy-done.19, bf16[80,256,128]{2,1,0:T(8,128)(2,1)} %gather_fusion, pred[80]{0:T(512)(128)(4,1)S(1)} %copy-done.37, s32[80,128,128]{2,1,0:T(8,128)} %param.38), kind=kOutput, calls=%fused_computation.8 | convolution fusion | flops 677642240 | bytes 21053520 | tf_op jit(solution)/shard_map/ctj,tjk->ctk/dot_general | solution.py:118
  130.1 9.4 %fusion.78 = bf16[256,8,128]{2,1,0:T(8,128)(2,1)S(1)} fusion(f32[256,8,128]{2,1,0:T(8,128)S(1)} %get-tuple-element.12, f32[8,256,128]{2,0,1:T(8,128)S(1)} %copy-done.15, f32[256,80,128]{2,0,1:T(8,128)S(1)} %bitcast_multiply_fusion.2, s32[80]{0:T(128)S(1)} %copy-done.43), kind=kOutput, calls=%fused_computation.76 | convolution fusion | flops 252445312 | bytes 13107520 | tf_op jit(solution)/shard_map/ctk,tb->cbk/dot_general | solution.py:122
  145.9 4.4 multiply_bitcast_fusion.1
  162.6 5.4 %collective-permute-start.2 = (bf16[256,1024]{0,1:T(8,128)(2,1)}, bf16[256,1024]{0,1:T(8,128)(2,1)}, u32[]{:S(2)}, u32[]{:S(2)}) collective-permute-start(bf16[256,1024]{0,1:T(8,128)(2,1)} %copy.184), channel_id=1, source_target_pairs={{0,4},{4,8},{8,12},{12,16},{16,20},{20,24},{24,28},{1,5},{5,9},{9,... | collective-permute-start | bytes 1572872 | tf_op jit(solution)/shard_map/ppermute | solution.py:18
  168.0 52.6 %reduce-scatter.6.cloned.1.call-done = f32[16,256]{1,0:T(8,128)} async-done(((f32[128,256]{1,0:T(8,128)}), f32[16,256]{1,0:T(8,128)}) %reduce-scatter.6.cloned.1.call-update) | async-done | bytes 16400 | tf_op jit(solution)/shard_map/reduce_scatter | solution.py:154
  225.9 32.4 %all_gather.6 = bf16[128,256]{1,0:T(8,128)(2,1)} all-gather(bf16[16,256]{1,0:T(8,128)(2,1)S(1)} %reshape.378), channel_id=1, replica_groups=mesh['ent'=8,'qry'=4] {'ent'}, dimensions={0}, use_global_device_ids=true | all-gather | bytes 73728 | tf_op jit(solution)/shard_map/all_gather | solution.py:124
  260.7 32.4 %all_gather.7 = bf16[128,256]{1,0:T(8,128)(2,1)} all-gather(bf16[16,256]{1,0:T(8,128)(2,1)S(1)} %reshape.382), channel_id=1, replica_groups=mesh['ent'=8,'qry'=4] {'ent'}, dimensions={0}, use_global_device_ids=true | all-gather | bytes 73728 | tf_op jit(solution)/shard_map/all_gather | solution.py:124
  296.5 3.8 fusion.26
  308.2 5.9 %gather_fusion.1 = bf16[80,256,128]{2,1,0:T(8,128)(2,1)} fusion(bf16[256,24,128]{2,0,1:T(8,128)(2,1)S(1)} %pad_maximum_fusion.1, s32[1024]{0:T(1024)} %pad_clamp_fusion.1), kind=kCustom, calls=%fused_computation.2.clone | custom fusion | bytes 10486080 | tf_op jit(solution)/shard_map/jit(_take)/gather | solution.py:117
  314.2 6.5 %bitcast_multiply_fusion.1 = f32[256,80,128]{2,0,1:T(8,128)S(1)} fusion(f32[256,80]{0,1:T(8,128)S(1)} %copy-done.18, bf16[80,256,128]{2,1,0:T(8,128)(2,1)} %gather_fusion.1, pred[80]{0:T(512)(128)(4,1)S(1)} %copy-done.38, s32[80,128,128]{2,1,0:T(8,128)} %param.38), kind=kOutput, calls=%fused_computation.7 | convolution fusion | flops 677642240 | bytes 21053520 | tf_op jit(solution)/shard_map/ctj,tjk->ctk/dot_general | solution.py:118
  320.8 9.4 %fusion.81 = bf16[256,8,128]{2,1,0:T(8,128)(2,1)S(1)} fusion(f32[256,8,128]{2,1,0:T(8,128)S(1)} %get-tuple-element.12, f32[8,256,128]{2,0,1:T(8,128)S(1)} %copy-done.17, f32[256,80,128]{2,0,1:T(8,128)S(1)} %bitcast_multiply_fusion.1, s32[80]{0:T(128)S(1)} %copy-done.44), kind=kOutput, calls=%fused_computation.77 | convolution fusion | flops 252445312 | bytes 13107520 | tf_op jit(solution)/shard_map/ctk,tb->cbk/dot_general | solution.py:122
  336.2 4.2 multiply_bitcast_fusion
  347.8 5.7 %fusion.24 = f32[8,256,128]{2,0,1:T(8,128)} fusion(f32[256,24,128]{2,0,1:T(8,128)} %bitcast_multiply_fusion.3, s32[24]{0:T(128)S(1)} %copy-done.48), kind=kOutput, calls=%fused_computation.30 | convolution fusion | flops 75497664 | bytes 4194400 | tf_op jit(solution)/shard_map/ctk,tb->cbk/dot_general | solution.py:133
  355.0 4.6 collective-permute-start.4
  359.6 49.4 %reduce-scatter.8.cloned.1.call-done = f32[16,256]{1,0:T(8,128)} async-done(((f32[128,256]{1,0:T(8,128)}), f32[16,256]{1,0:T(8,128)}) %reduce-scatter.8.cloned.1.call-update) | async-done | bytes 16400 | tf_op jit(solution)/shard_map/reduce_scatter | solution.py:154
  413.6 5.8 %gather_fusion.3 = bf16[80,256,128]{2,1,0:T(8,128)(2,1)} fusion(bf16[256,24,128]{2,0,1:T(8,128)(2,1)S(1)} %pad_maximum_fusion.2, s32[1024]{0:T(1024)} %pad_clamp_fusion.1), kind=kCustom, calls=%fused_computation.3.clone | custom fusion | bytes 10486080 | tf_op jit(solution)/shard_map/jit(_take)/gather | solution.py:117
  419.4 6.6 %bitcast_multiply_fusion = f32[256,80,128]{2,0,1:T(8,128)S(1)} fusion(f32[256,80]{0,1:T(8,128)S(1)} %copy.203, bf16[80,256,128]{2,1,0:T(8,128)(2,1)} %gather_fusion.3, pred[80]{0:T(512)(128)(4,1)S(1)} %copy-done.38, s32[80,128,128]{2,1,0:T(8,128)} %param.38), kind=kOutput, calls=%fused_computation.6 | convolution fusion | flops 677642240 | bytes 21053520 | tf_op jit(solution)/shard_map/ctj,tjk->ctk/dot_general | solution.py:118
  426.1 9.4 %fusion.84 = bf16[256,8,128]{2,1,0:T(8,128)(2,1)S(1)} fusion(f32[256,8,128]{2,1,0:T(8,128)S(1)} %get-tuple-element.12, f32[8,256,128]{2,0,1:T(8,128)S(1)} %copy-done.16, f32[256,80,128]{2,0,1:T(8,128)S(1)} %bitcast_multiply_fusion, s32[80]{0:T(128)S(1)} %copy-done.45), kind=kOutput, calls=%fused_computation.78 | convolution fusion | flops 252445312 | bytes 13107520 | tf_op jit(solution)/shard_map/ctk,tb->cbk/dot_general | solution.py:122
  443.8 7.6 %all-to-all-done = bf16[4,2,32768]{2,1,0:T(2,128)(2,1)S(1)} async-done(((bf16[4,2,32768]{2,1,0:T(2,128)(2,1)}), bf16[4,2,32768]{2,1,0:T(2,128)(2,1)S(1)}, u32[]{:S(2)}, u32[]{:S(2)}) %all-to-all-start) | async-done | bytes 524320 | tf_op jit(solution)/shard_map/all_to_all | solution.py:175
  (278 shorter events, 115.4 us)
Async XLA Ops:
  7.2 105.1 %reduce-scatter.4.cloned.1.call-start = ((), (), s32[]{:S(2)}) async-start(), calls=%async_computation.4 | async-start | bytes 147456 | tf_op jit(solution)/shard_map/reduce_scatter | solution.py:154
  12.1 102.5 %collective-permute-start.1 = (bf16[256,1024]{1,0:T(8,128)(2,1)}, bf16[256,1024]{1,0:T(8,128)(2,1)}, u32[]{:S(2)}, u32[]{:S(2)}) collective-permute-start(bf16[256,1024]{1,0:T(8,128)(2,1)} %fusion.90), channel_id=1, source_target_pairs={{4,0},{8,4},{12,8},{16,12},{20,16},{24,20},{28,24},{5,1},{9,5},{13... | collective-permute-start | bytes 1572872 | tf_op jit(solution)/shard_map/ppermute | solution.py:20
  13.4 102.4 %collective-permute-start = (bf16[256,1024]{1,0:T(8,128)(2,1)}, bf16[256,1024]{1,0:T(8,128)(2,1)}, u32[]{:S(2)}, u32[]{:S(2)}) collective-permute-start(bf16[256,1024]{1,0:T(8,128)(2,1)} %fusion.90), channel_id=1, source_target_pairs={{0,4},{4,8},{8,12},{12,16},{16,20},{20,24},{24,28},{1,5},{5,9},{9,... | collective-permute-start | bytes 1572872 | tf_op jit(solution)/shard_map/ppermute | solution.py:18
  45.5 8.8 %copy-start.61 = (s32[80,2]{0,1:T(2,128)S(1)}, s32[80,2]{0,1:T(2,128)}, u32[]{:S(2)}) copy-start(s32[80,2]{0,1:T(2,128)} %param.36) | copy-start | bytes 1924
  45.5 9.2 %copy-start.4 = (s32[24,128,128]{2,1,0:T(8,128)S(1)}, s32[24,128,128]{2,1,0:T(8,128)}, u32[]{:S(2)}) copy-start(s32[24,128,128]{2,1,0:T(8,128)} %param.44) | copy-start | bytes 4718596
  49.4 171.2 %reduce-scatter.6.cloned.1.call-start = ((), (), s32[]{:S(2)}) async-start(), calls=%async_computation.5 | async-start | bytes 147456 | tf_op jit(solution)/shard_map/reduce_scatter | solution.py:154
  50.2 9.7 %copy-start.46 = (s32[24]{0:T(128)}, s32[24]{0:T(128)S(1)}, u32[]{:S(2)}) copy-start(s32[24]{0:T(128)S(1)} %subtract_bitcast_fusion) | copy-start | bytes 292
  54.3 58.8 %copy-start.50 = (f32[64]{0:T(128)}, f32[64]{0:T(128)S(1)}, u32[]{:S(2)}) copy-start(f32[64]{0:T(128)S(1)} %get-tuple-element.22) | copy-start | bytes 772
  56.0 60.8 %copy-start.14 = (bf16[256,8,128]{2,1,0:T(8,128)(2,1)S(1)}, bf16[256,8,128]{2,1,0:T(8,128)(2,1)}, u32[]{:S(2)}) copy-start(bf16[256,8,128]{2,1,0:T(8,128)(2,1)} %copy-done.13) | copy-start | bytes 1572868
  60.7 51.6 %copy-start.29 = (f32[16,64]{1,0:T(8,128)}, f32[16,64]{1,0:T(8,128)S(1)}, u32[]{:S(2)}) copy-start(f32[16,64]{1,0:T(8,128)S(1)} %convolution_add_fusion.8) | copy-start | bytes 12292
  130.1 9.6 %copy-start.51 = (f32[64]{0:T(128)S(1)}, f32[64]{0:T(128)}, u32[]{:S(2)}) copy-start(f32[64]{0:T(128)} %copy-done.50) | copy-start | bytes 772
  153.9 140.8 %copy-start.5 = (s32[24,128,128]{2,1,0:T(8,128)S(1)}, s32[24,128,128]{2,1,0:T(8,128)}, u32[]{:S(2)}) copy-start(s32[24,128,128]{2,1,0:T(8,128)} %param.44) | copy-start | bytes 4718596
  157.9 251.2 %reduce-scatter.8.cloned.1.call-start = ((), (), s32[]{:S(2)}) async-start(), calls=%async_computation.6 | async-start | bytes 147456 | tf_op jit(solution)/shard_map/reduce_scatter | solution.py:154
  161.3 141.4 %collective-permute-start.3 = (bf16[256,1024]{0,1:T(8,128)(2,1)}, bf16[256,1024]{0,1:T(8,128)(2,1)}, u32[]{:S(2)}, u32[]{:S(2)}) collective-permute-start(bf16[256,1024]{0,1:T(8,128)(2,1)} %copy.184), channel_id=1, source_target_pairs={{4,0},{8,4},{12,8},{16,12},{20,16},{24,20},{28,24},{5,1},{9,5},{13... | collective-permute-start | bytes 1572872 | tf_op jit(solution)/shard_map/ppermute | solution.py:20
  162.6 142.2 %collective-permute-start.2 = (bf16[256,1024]{0,1:T(8,128)(2,1)}, bf16[256,1024]{0,1:T(8,128)(2,1)}, u32[]{:S(2)}, u32[]{:S(2)}) collective-permute-start(bf16[256,1024]{0,1:T(8,128)(2,1)} %copy.184), channel_id=1, source_target_pairs={{0,4},{4,8},{8,12},{12,16},{16,20},{20,24},{24,28},{1,5},{5,9},{9,... | collective-permute-start | bytes 1572872 | tf_op jit(solution)/shard_map/ppermute | solution.py:18
  225.8 70.6 %copy-start.47 = (s32[24]{0:T(128)S(1)}, s32[24]{0:T(128)}, u32[]{:S(2)}) copy-start(s32[24]{0:T(128)} %copy-done.46) | copy-start | bytes 292
  343.9 9.5 %copy-start.10 = (bf16[4,64,1024]{2,1,0:T(8,128)(2,1)S(1)}, bf16[4,64,1024]{2,1,0:T(8,128)(2,1)}, u32[]{:S(2)}) copy-start(bf16[4,64,1024]{2,1,0:T(8,128)(2,1)} %copy-done.9) | copy-start | bytes 1572868
  347.1 62.7 %copy-start.21 = (bf16[3,64,64]{2,1,0:T(8,128)(2,1)S(1)}, bf16[3,64,64]{2,1,0:T(8,128)(2,1)}, u32[]{:S(2)}) copy-start(bf16[3,64,64]{2,1,0:T(8,128)(2,1)} %param.32) | copy-start | bytes 73732
  347.1 62.7 %copy-start.49 = (f32[64]{0:T(128)S(1)}, f32[64]{0:T(128)}, u32[]{:S(2)}) copy-start(f32[64]{0:T(128)} %get-tuple-element.21) | copy-start | bytes 772
  353.7 56.5 %collective-permute-start.5 = (bf16[256,1024]{0,1:T(8,128)(2,1)S(1)}, bf16[256,1024]{0,1:T(8,128)(2,1)S(1)}, u32[]{:S(2)}, u32[]{:S(2)}) collective-permute-start(bf16[256,1024]{0,1:T(8,128)(2,1)S(1)} %copy.198), channel_id=1, source_target_pairs={{4,0},{8,4},{12,8},{16,12},{20,16},{24,20},{28,24},{5,1},{9,5},{13... | collective-permute-start | bytes 1572872 | tf_op jit(solution)/shard_map/ppermute | solution.py:20
  355.0 56.3 %collective-permute-start.4 = (bf16[256,1024]{0,1:T(8,128)(2,1)S(1)}, bf16[256,1024]{0,1:T(8,128)(2,1)S(1)}, u32[]{:S(2)}, u32[]{:S(2)}) collective-permute-start(bf16[256,1024]{0,1:T(8,128)(2,1)S(1)} %copy.198), channel_id=1, source_target_pairs={{0,4},{4,8},{8,12},{12,16},{16,20},{20,24},{24,28},{1,5},{5,9},{9,... | collective-permute-start | bytes 1572872 | tf_op jit(solution)/shard_map/ppermute | solution.py:18
  437.6 15.1 %copy-start.30 = (f32[16,64]{1,0:T(8,128)S(1)}, f32[16,64]{1,0:T(8,128)}, u32[]{:S(2)}) copy-start(f32[16,64]{1,0:T(8,128)} %copy-done.29) | copy-start | bytes 12292
  439.2 12.3 %all-to-all-start = ((bf16[4,2,32768]{2,1,0:T(2,128)(2,1)}), bf16[4,2,32768]{2,1,0:T(2,128)(2,1)S(1)}, u32[]{:S(2)}, u32[]{:S(2)}) async-start(bf16[4,2,32768]{2,1,0:T(2,128)(2,1)} %reshape.477), calls=%async_computation.2 | async-start | bytes 1048576 | tf_op jit(solution)/shard_map/all_to_all | solution.py:175
  442.7 11.6 %copy-start.1 = (bf16[822,64]{0,1:T(8,128)(2,1)S(1)}, bf16[822,64]{0,1:T(8,128)(2,1)}, u32[]{:S(2)}) copy-start(bf16[822,64]{0,1:T(8,128)(2,1)} %param.30) | copy-start | bytes 315652
  (50 other events, 188.3 us)
Sparse Core Ops, SparseCore 0:
  49.6 62.6 reduce-scatter.3
  158.0 62.5 reduce-scatter.5
  347.9 61.0 reduce-scatter.7
where the time goes:
time: 468 us; the launch traced here: 461 us
  waiting for transfers between devices  158 us (34%)
  matrix products  107 us (23%)
  local copies, waits for them, and re-layouts  71.9 us (15%)
  blocking collectives  64.8 us (14%)
  starting transfers between devices  23.9 us (5%)
  other arithmetic  20.6 us (4%)
  between operations  15.3 us (3%)
    reduce_scatter x3, waiting for transfers between devices, body(): lax.psum_scatter(partial_value, 'ent', scatter_dimension=0, tiled=True)  150 us
    all_gather x2, blocking collectives, body(): hub_full = lax.all_gather(hub_own, 'ent', axis=0, tiled=True)  64.8 us
    dot_general x3, matrix products, body(): totals = jnp.einsum('ctk,tb->cbk', product, reg_onehot, precision=highest)  28.1 us
    dot_general x3, matrix products, body(): jnp.einsum('ctj,tjk->ctk', gathered, reg_masks, preferred_element_type=jn...  19.8 us
    gather x3, local copies, waits for them, and re-layouts, body(): gathered = jnp.take(window_blocks, reg_sources, axis=1)  17.7 us
    ppermute x3, starting transfers between devices, padded(): lax.ppermute(tail, axis, [(i, (i + 1) % count) for i in range(ends)])  16.3 us
    dot_general x3, matrix products, body(): jnp.einsum('ctk,tb->cbk', product, hout_onehot, precision=highest)  13.3 us
    dot_general x3, matrix products, body(): jnp.einsum('ctj,tjk->tkc', hin_gathered, hin_masks, preferred_element_typ...  12.6 us
  transfers between devices with their start and end apart: 10, of which 4 were waited for; matrix products, arithmetic and copies ran while one was open for 17% of the time, Pallas kernels for 0%

commit v1 on v0

v1 whole, which is shorter than its diff:
```python
import functools

import jax
import jax.numpy as jnp
from jax import lax
from jax.experimental import pallas as pl
from jax.experimental.pallas import tpu as pltpu
from jax.sharding import PartitionSpec as P

HUB_DEV = 16
JOIN = 4
F32 = jnp.float32
BF16 = jnp.bfloat16
SMEM = pl.BlockSpec(memory_space=pltpu.SMEM)
VMEM = pl.BlockSpec(memory_space=pltpu.VMEM)
LEFT, OWN, RIGHT, HOUT, HIN = range(5)


class Plan:
    def __init__(self, tiles, blocks, hub_blocks):
        self.tiles = tiles
        self.keys = 4 * blocks + hub_blocks
        self.chunks = tiles // JOIN + self.keys
        self.target = 8
        self.tile = self.target + self.chunks
        self.source = self.tile + self.chunks * JOIN
        self.size = self.source + self.chunks * JOIN


def prep_kernel(
    plan, blocks, hub_blocks, splits, layers,
    reg_blocks, hin_blocks, hout_blocks, reg_rel, hin_rel, hout_rel, query_rel, query_head,
    query_table, rel_table, read_weight, read_bias, reg_mask, hin_mask, hout_mask,
    turned, rel_rows, lane_rows, lane_heads, order, table, rows, q_rows, key_of, source_of, count_of, slot_of,
):
    step = pl.program_id(0)
    tiles_reg, tiles_hin = reg_rel.shape[0], hin_rel.shape[0]
    tiles_hout = hout_rel.shape[0]
    q_local, width = q_rows.shape[0] - 4, query_table.shape[1]
    lanes = lane_rows.shape[1]

    @pl.when(step == 0)
    def _():
        first_block = lax.axis_index("ent") * blocks
        query_first = lax.axis_index("qry") * q_local

        def clear(k, _):
            count_of[k] = 0
            return 0

        lax.fori_loop(0, plan.keys, clear, 0)

        def note(tile, key, source):
            key_of[tile] = key
            source_of[tile] = source
            count_of[key] = count_of[key] + 1

        def note_reg(t, _):
            place = reg_blocks[t, 1] - first_block + blocks
            side = lax.div(place, blocks)
            note(t, side * blocks + reg_blocks[t, 0] - first_block, place - side * blocks)
            return 0

        def note_hin(t, _):
            note(tiles_reg + t, 4 * blocks + hin_blocks[t, 0], hin_blocks[t, 1] - first_block)
            return 0

        def note_hout(t, _):
            note(
                tiles_reg + tiles_hin + t,
                3 * blocks + hout_blocks[t, 0] - first_block,
                hout_blocks[t, 1],
            )
            return 0

        lax.fori_loop(0, tiles_reg, note_reg, 0)
        lax.fori_loop(0, tiles_hin, note_hin, 0)
        lax.fori_loop(0, tiles_hout, note_hout, 0)

        chunk = jnp.int32(0)
        for side in range(5):
            order[side] = chunk
            keys = hub_blocks if side == HIN else blocks

            def lay(k, chunk, side=side):
                key = side * blocks + k
                slot_of[key] = chunk * JOIN
                need = lax.div(count_of[key] + (JOIN - 1), JOIN)

                def fill(c, _):
                    order[plan.target + c] = k
                    for u in range(JOIN):
                        order[plan.tile + c * JOIN + u] = plan.tiles
                        order[plan.source + c * JOIN + u] = 0
                    return 0

                lax.fori_loop(chunk, chunk + need, fill, 0)
                return chunk + need

            chunk = lax.fori_loop(0, keys, lay, chunk)
        order[5] = chunk

        def put(t, _):
            key = key_of[t]
            slot = slot_of[key]
            order[plan.tile + slot] = t
            order[plan.source + slot] = source_of[t]
            slot_of[key] = slot + 1
            return 0

        lax.fori_loop(0, plan.tiles, put, 0)

        table[...] = rel_table[...].astype(F32)
        rows[...] = jnp.zeros_like(rows)

        def rel_put(base, ref):
            def one(t, _):
                for layer in range(layers):
                    rows[layer, pl.ds(base + t, 1), :] = table[layer, pl.ds(ref[t], 1), :]
                return 0

            return one

        lax.fori_loop(0, tiles_reg, rel_put(0, reg_rel), 0)
        lax.fori_loop(0, tiles_hin, rel_put(tiles_reg, hin_rel), 0)
        lax.fori_loop(0, tiles_hout, rel_put(tiles_reg + tiles_hin, hout_rel), 0)
        spread = spreader(width, lanes)
        for layer in range(layers):
            rel_rows[layer] = jnp.dot(rows[layer].astype(BF16), spread, preferred_element_type=F32)

        table[0] = query_table[...].astype(F32)
        q_rows[...] = jnp.zeros_like(q_rows)
        for q in range(q_local):
            q_rows[pl.ds(q, 1), :] = table[0, pl.ds(query_rel[query_first + q], 1), :]
        own = q_rows[...].astype(BF16)
        parts = jnp.dot(own, read_weight[width:, :], preferred_element_type=F32) + read_bias[...]
        q_of_lane = lax.div(lax.broadcasted_iota(jnp.int32, (1, lanes), 1), width)
        values = jnp.dot(own, spread, preferred_element_type=F32)
        part_values = jnp.dot(parts, spread.astype(F32), precision=lax.Precision.HIGHEST)
        lane_q = jnp.zeros((1, lanes), F32)
        lane_part = jnp.zeros((1, lanes), F32)
        lane_head = jnp.zeros((1, lanes), jnp.int32)
        for q in range(q_local):
            lane_q = jnp.where(q_of_lane == q, values[q : q + 1, :], lane_q)
            lane_part = jnp.where(q_of_lane == q, part_values[q : q + 1, :], lane_part)
            lane_head = jnp.where(q_of_lane == q, query_head[query_first + q], lane_head)
        lane_rows[...] = jnp.zeros_like(lane_rows)
        lane_rows[0:1, :] = lane_q
        lane_rows[1:2, :] = lane_part
        lane_heads[...] = jnp.broadcast_to(lane_head, lane_heads.shape)

    def turn(mask):
        for t in range(mask.shape[0]):
            turned[t] = jnp.transpose(mask[t].astype(F32)).astype(BF16)

    pl.when(step < splits[0])(lambda: turn(reg_mask))
    pl.when((step >= splits[0]) & (step < splits[1]))(lambda: turn(hin_mask))
    pl.when(step >= splits[1])(lambda: turn(hout_mask))


def spreader(width, lanes):
    row = lax.broadcasted_iota(jnp.int32, (width, lanes), 0)
    column = lax.broadcasted_iota(jnp.int32, (width, lanes), 1)
    return (lax.rem(column, width) == row).astype(F32).astype(BF16)


def group_mean_matrix(width, lanes):
    row = lax.broadcasted_iota(jnp.int32, (lanes, lanes), 0)
    column = lax.broadcasted_iota(jnp.int32, (lanes, lanes), 1)
    same = lax.div(row, width) == lax.div(column, width)
    return jnp.where(same, 1.0 / width, 0.0).astype(BF16)


def split_dot(values, matrix):
    high = values.astype(BF16)
    low = (values - high.astype(F32)).astype(BF16)
    return jnp.dot(high, matrix, preferred_element_type=F32) + jnp.dot(
        low, matrix, preferred_element_type=F32
    )


def run_tiles(plan, side, order, turned, rel_row, source, total):
    block = turned.shape[1]
    lanes = total.shape[1]

    def chunk(c, _):
        masks, values = [], []
        for u in range(JOIN):
            tile = order[plan.tile + c * JOIN + u]
            start = pl.multiple_of(order[plan.source + c * JOIN + u] * block, block)
            row = jnp.broadcast_to(rel_row[pl.ds(tile, 1), :], (16, lanes)).astype(BF16)
            value = source[pl.ds(start, block), :].reshape(block // 16, 16, lanes)
            values.append((value * row[None]).reshape(block, lanes))
            masks.append(turned[jnp.minimum(tile, plan.tiles - 1)])
        product = jnp.dot(
            jnp.concatenate(masks, axis=1),
            jnp.concatenate(values, axis=0),
            preferred_element_type=F32,
        )
        place = pl.ds(pl.multiple_of(order[plan.target + c] * block, block), block)
        total[place, :] += product
        return 0

    lax.fori_loop(order[side], order[side + 1], chunk, 0)


def normed_step(inputs, weight, means, bias, gain, shift):
    linear = jnp.dot(inputs, weight, preferred_element_type=F32) + bias
    centered = linear - split_dot(linear, means)
    variance = split_dot(centered * centered, means)
    return jnp.maximum(centered * lax.rsqrt(variance + 1e-05) * gain + shift, 0.0)


def hit_lanes(rows, first, heads, values):
    place = first + lax.broadcasted_iota(jnp.int32, (rows, heads.shape[1]), 0)
    return jnp.where(place == heads, values, 0.0)


def first_states(feat, first, lane_rows, lane_heads, out):
    width, count = feat.shape
    lanes = out.shape[1]
    columns = jnp.transpose(feat[...].astype(F32)).astype(BF16)
    spread = spreader(width, lanes)
    block = 128
    for start in range(0, count, block):
        wide = jnp.dot(columns[start : start + block, :], spread, preferred_element_type=F32)
        hits = hit_lanes(block, first + start, lane_heads[0:1, :], lane_rows[0:1, :])
        out[start : start + block, :] = (wide + hits).astype(BF16)


def own_kernel(plan, layer, order, turned, rel_row, *refs):
    if layer == 0:
        feat, lane_rows, lane_heads, states, total, hub_part = refs
        first = lax.axis_index("ent") * feat.shape[1]
        first_states(feat, first, lane_rows, lane_heads, states)
    else:
        states, total, hub_part = refs
    hub_part[...] = jnp.zeros_like(hub_part)
    total[...] = jnp.zeros_like(total)
    run_tiles(plan, HIN, order, turned, rel_row, states, hub_part)
    run_tiles(plan, OWN, order, turned, rel_row, states, total)


def update_hubs(hub_sum, hub_old, lane_rows, params, weight, means, layer, layers):
    inputs = (hub_sum * lane_rows[0:1, :]).astype(BF16)
    grown = normed_step(
        inputs, weight, means, params[layer : layer + 1, :],
        params[layers + layer : layers + layer + 1, :],
        params[2 * layers + layer : 2 * layers + layer + 1, :],
    )
    if hub_old is None:
        return grown.astype(BF16)
    return (grown + hub_old.astype(F32)).astype(BF16)


def score_rows(values, weight, lane_part, picks):
    features = jnp.maximum(jnp.dot(values, weight, preferred_element_type=F32) + lane_part, 0.0)
    high = features.astype(BF16)
    low = (features - high.astype(F32)).astype(BF16)
    pick_high = picks.astype(BF16)
    pick_low = (picks - pick_high.astype(F32)).astype(BF16)

    def across(a, b):
        return lax.dot_general(a, b, (((1,), (1,)), ((), ())), preferred_element_type=F32)

    return across(pick_high, high) + across(pick_high, low) + across(pick_low, high)


def pick_matrix(read_row, width, lanes):
    row = lax.broadcasted_iota(jnp.int32, (8, lanes), 0)
    column = lax.broadcasted_iota(jnp.int32, (8, lanes), 1)
    return jnp.where(lax.div(column, width) == row, read_row, 0.0)


def close_kernel(plan, layer, layers, width, order, turned, rel_row, own, total_in, lane_rows, lane_heads, params, weights, *refs):
    last = layer == layers - 1
    lanes = own.shape[1]
    count = own.shape[0]
    first = lax.axis_index("ent") * count
    means = group_mean_matrix(width, lanes)
    if layer == 0:
        left_feat, right_feat, states, total, left, right = refs
        first_states(left_feat, first - count, lane_rows, lane_heads, left)
        first_states(right_feat, first + count, lane_rows, lane_heads, right)
        total[...] = total_in[...]
    else:
        if layer == 1:
            left, right, hub_sum, states, hub_new, total = refs
            hub_old = None
        else:
            left, right, hub_sum, hub_old_ref, states, hub_new, total = refs
            hub_old = hub_old_ref[...]
        hub_new[...] = update_hubs(
            hub_sum[...], hub_old, lane_rows, params, weights[layer - 1], means, layer - 1, layers
        )
        total[...] = total_in[...]
        run_tiles(plan, HOUT, order, turned, rel_row, hub_new, total)
    run_tiles(plan, LEFT, order, turned, rel_row, left, total)
    run_tiles(plan, RIGHT, order, turned, rel_row, right, total)
    weight = weights[layer]
    block = 128
    lane_q = lane_rows[0:1, :]
    for start in range(0, count, block):
        place = slice(start, start + block)
        hits = hit_lanes(block, first + start, lane_heads[0:1, :], lane_q)
        inputs = (total[place, :] * lane_q + hits).astype(BF16)
        grown = normed_step(
            inputs, weight, means, params[layer : layer + 1, :],
            params[layers + layer : layers + layer + 1, :],
            params[2 * layers + layer : 2 * layers + layer + 1, :],
        )
        new = (grown + own[place, :].astype(F32)).astype(BF16)
        if last:
            picks = pick_matrix(params[3 * layers : 3 * layers + 1, :], width, lanes)
            states[:, place] = score_rows(new, weights[layers], lane_rows[1:2, :], picks)
        else:
            states[place, :] = new


def hub_kernel(layers, width, hub_sum, hub_old, lane_rows, params, weights, out):
    lanes = hub_sum.shape[1]
    means = group_mean_matrix(width, lanes)
    new = update_hubs(
        hub_sum[...], hub_old[...], lane_rows, params, weights[layers - 1], means, layers - 1, layers
    )
    picks = pick_matrix(params[3 * layers : 3 * layers + 1, :], width, lanes)
    out[...] = score_rows(new, weights[layers], lane_rows[1:2, :], picks)


def body(
    ent_feat, query_head, query_rel, query_table, rel_table, layer_weight, layer_bias, norm_gain,
    norm_shift, reg_blocks, reg_rel, reg_mask, hin_blocks, hin_rel, hin_mask, hout_blocks,
    hout_rel, hout_mask, read_weight, read_bias, read_out,
):
    ends = lax.axis_size("ent")
    layers = rel_table.shape[0]
    q_local = query_head.shape[0] // lax.axis_size("qry")
    width, ent_local = ent_feat.shape
    block = reg_mask.shape[1]
    blocks = ent_local // block
    hubs = HUB_DEV * ends
    hub_blocks = hubs // block
    lanes = q_local * width
    counts = [reg_mask.shape[0], hin_mask.shape[0], hout_mask.shape[0]]
    tiles = sum(counts)
    plan = Plan(tiles, blocks, hub_blocks)
    padded = tiles + 8
    relations = rel_table.shape[1]

    group = 8
    while any(c % group for c in counts):
        group //= 2
    steps = [c // group for c in counts]
    splits = (steps[0], steps[0] + steps[1])

    def mask_spec(offset, length):
        return pl.BlockSpec(
            (group, block, block), lambda i: (jnp.clip(i - offset, 0, length - 1), 0, 0)
        )

    def whole(shape):
        return pl.BlockSpec(shape, lambda i: (0,) * len(shape))

    turned, rel_rows, lane_rows, lane_heads, order = pl.pallas_call(
        functools.partial(prep_kernel, plan, blocks, hub_blocks, splits, layers),
        grid=(sum(steps),),
        in_specs=[SMEM] * 8
        + [whole(query_table.shape), whole(rel_table.shape), whole(read_weight.shape), whole((1, width))]
        + [mask_spec(0, steps[0]), mask_spec(splits[0], steps[1]), mask_spec(splits[1], steps[2])],
        out_specs=[
            pl.BlockSpec((group, block, block), lambda i: (i, 0, 0)),
            whole((layers, padded, lanes)),
            whole((8, lanes)),
            whole((8, lanes)),
            SMEM,
        ],
        out_shape=[
            jax.ShapeDtypeStruct((tiles, block, block), BF16),
            jax.ShapeDtypeStruct((layers, padded, lanes), F32),
            jax.ShapeDtypeStruct((8, lanes), F32),
            jax.ShapeDtypeStruct((8, lanes), jnp.int32),
            jax.ShapeDtypeStruct((plan.size,), jnp.int32),
        ],
        scratch_shapes=[
            pltpu.VMEM((layers, relations, width), F32),
            pltpu.VMEM((layers, padded, width), F32),
            pltpu.VMEM((q_local + 4, width), F32),
            pltpu.SMEM((tiles,), jnp.int32),
            pltpu.SMEM((tiles,), jnp.int32),
            pltpu.SMEM((plan.keys,), jnp.int32),
            pltpu.SMEM((plan.keys,), jnp.int32),
        ],
        cost_estimate=pl.CostEstimate(
            flops=0, bytes_accessed=tiles * block * block * 6, transcendentals=0
        ),
        name="prep",
    )(
        reg_blocks, hin_blocks, hout_blocks, reg_rel, hin_rel, hout_rel, query_rel, query_head,
        query_table, rel_table, read_weight, read_bias[None, :], reg_mask, hin_mask, hout_mask,
    )

    params = jnp.tile(
        jnp.concatenate([layer_bias, norm_gain, norm_shift, read_out[None, :]], axis=0), (1, q_local)
    )
    same = jnp.arange(lanes)[:, None] // width == jnp.arange(lanes)[None, :] // width
    square = jnp.concatenate([layer_weight, read_weight[None, :width]], axis=0)
    weights = jnp.where(same[None], jnp.tile(square, (1, q_local, q_local)), jnp.zeros((), BF16))

    def shifts(cells):
        left = lax.ppermute(cells, "ent", [(i, i + 1) for i in range(ends - 1)])
        right = lax.ppermute(cells, "ent", [(i + 1, i) for i in range(ends - 1)])
        return left, right

    def summed(part):
        stride = 1
        while stride < ends:
            part = part + lax.ppermute(part, "ent", [(i, i ^ stride) for i in range(ends)])
            stride *= 2
        return part

    def call(kernel, name, operands, outs, scratch=(), tile_count=0):
        return pl.pallas_call(
            kernel,
            in_specs=[SMEM] + [VMEM] * (len(operands) - 1) if name != "hubs" else [VMEM] * len(operands),
            out_specs=[VMEM] * len(outs),
            out_shape=outs,
            scratch_shapes=list(scratch),
            cost_estimate=pl.CostEstimate(
                flops=2 * tile_count * block * block * lanes,
                bytes_accessed=4 * tile_count * block * block,
                transcendentals=0,
            ),
            name=name,
        )(*operands)

    state_shape = jax.ShapeDtypeStruct((ent_local, lanes), BF16)
    total_shape = jax.ShapeDtypeStruct((ent_local, lanes), F32)
    part_shape = jax.ShapeDtypeStruct((hubs, lanes), F32)
    hub_shape = jax.ShapeDtypeStruct((hubs, lanes), BF16)
    score_shape = jax.ShapeDtypeStruct((8, ent_local), F32)
    total_scratch = pltpu.VMEM((ent_local, lanes), F32)
    state_scratch = pltpu.VMEM((ent_local, lanes), BF16)

    left, right = shifts(ent_feat)
    states, total, part = call(
        functools.partial(own_kernel, plan, 0), "own",
        (order, turned, rel_rows[0], ent_feat, lane_rows, lane_heads),
        (state_shape, total_shape, part_shape), (), tiles // 2,
    )
    hub_old = None
    hub_sum = None
    for layer in range(layers):
        last = layer == layers - 1
        base = (order, turned, rel_rows[layer], states, total, lane_rows, lane_heads, params, weights)
        kernel = functools.partial(close_kernel, plan, layer, layers, width)
        next_sum = summed(part)
        out_shape = score_shape if last else state_shape
        if layer == 0:
            (states,) = call(
                kernel, "close", base + (left, right), (out_shape,),
                (total_scratch, state_scratch, state_scratch), tiles,
            )
        else:
            extra = (left, right, hub_sum) if layer == 1 else (left, right, hub_sum, hub_old)
            states, hub_old = call(
                kernel, "close", base + extra, (out_shape, hub_shape), (total_scratch,), tiles
            )
        hub_sum = next_sum
        if not last:
            left, right = shifts(states)
            total, part = call(
                functools.partial(own_kernel, plan, layer + 1), "own",
                (order, turned, rel_rows[layer + 1], states), (total_shape, part_shape), (), tiles // 2,
            )
    (hub_scores,) = call(
        functools.partial(hub_kernel, layers, width), "hubs",
        (hub_sum, hub_old, lane_rows, params, weights), (jax.ShapeDtypeStruct((8, hubs), F32),),
    )
    scores = lax.all_to_all(states[:q_local], "qry", split_axis=1, concat_axis=0, tiled=True)
    hub_scores = lax.dynamic_slice(
        hub_scores, (0, lax.axis_index("ent") * HUB_DEV), (q_local, HUB_DEV)
    )
    return scores, hub_scores


def solution(mesh):
    return jax.shard_map(
        body,
        mesh=mesh,
        in_specs=(
            P(None, "ent"), P(), P(), P(), P(), P(), P(), P(), P(),
            P("ent", None), P("ent"), P("ent", None, None),
            P("ent", None), P("ent"), P("ent", None, None),
            P("ent", None), P("ent"), P("ent", None, None),
            P(), P(), P(),
        ),
        out_specs=(P(None, ("ent", "qry")), P("qry", "ent")),
        check_vma=False,
    )
```

time: 468 us -> 193 us (0.41); the launches traced: 461 us -> 192 us
  waiting for transfers between devices: 158 us -> 47.5 us
  matrix products: 107 us -> 0 us
  Pallas kernels: 0 us -> 75.6 us
  blocking collectives: 64.8 us -> 0 us
  local copies, waits for them, and re-layouts: 71.9 us -> 19.7 us
  starting transfers between devices: 23.9 us -> 44.2 us
  other arithmetic: 20.6 us -> 4.02 us
  between operations: 15.3 us -> 0.88 us
    reduce_scatter x3 -> x0, waiting for transfers between devices: 150 us -> none  [body(): lax.psum_scatter(partial_value, 'ent', scatter_dimension=0, tiled=True)]
    dot_general x39 -> x0, matrix products: 107 us -> none  [the longest x3 28.1 us: body(): totals = jnp.einsum('ctk,tb->cbk', product, reg_onehot, precision=highest)]
    pallas_call x0 -> x8, Pallas kernels: none -> 75.6 us  [the longest x7 56.9 us: call(): pl.pallas_call(kernel, in_specs=[SMEM] + [VMEM] * (len(operands) - 1) if...]
    all_gather x2 -> x0, blocking collectives: 64.8 us -> none  [body(): hub_full = lax.all_gather(hub_own, 'ent', axis=0, tiled=True)]
    ppermute x6 -> x15, waiting for transfers between devices: 0.02 us -> 47.5 us  [the longest x9 47.5 us: summed(): lax.ppermute(part, 'ent', [(i, i ^ stride) for i in range(ends)])]
    gather x8 -> x0, local copies, waits for them, and re-layouts: 27 us -> none  [the longest x3 17.7 us: body(): gathered = jnp.take(window_blocks, reg_sources, axis=1)]
    ppermute x6 -> x15, starting transfers between devices: 20.1 us -> 41 us  [the longest x9 24 us: summed(): lax.ppermute(part, 'ent', [(i, i ^ stride) for i in range(ends)])]
    mul x20 -> x0, local copies, waits for them, and re-layouts: 14.9 us -> none  [the longest x3 10.7 us: body(): hin_product * tile_coefficients(hin_rel, rel_layer).T[:, None, :]]
  transfers between devices with their start and end apart: 10 -> 16, of which waited for: 4 -> 6; matrix products, arithmetic and copies ran while one was open for 17% -> 10% of each run, Pallas kernels for 0% -> 23%
where the time goes in v1:
time: 193 us; the launch traced here: 192 us
  Pallas kernels  75.6 us (39%)
  waiting for transfers between devices  47.5 us (25%)
  starting transfers between devices  44.2 us (23%)
  local copies, waits for them, and re-layouts  19.7 us (10%)
  other arithmetic  4.02 us (2%)
    pallas_call x7, Pallas kernels, call(): pl.pallas_call(kernel, in_specs=[SMEM] + [VMEM] * (len(operands) - 1) if...  56.9 us
    ppermute x9, waiting for transfers between devices, summed(): lax.ppermute(part, 'ent', [(i, i ^ stride) for i in range(ends)])  47.5 us
    ppermute x9, starting transfers between devices, summed(): lax.ppermute(part, 'ent', [(i, i ^ stride) for i in range(ends)])  24 us
    pallas_call x1, Pallas kernels, body(): pl.pallas_call(functools.partial(prep_kernel, plan, blocks, hub_blocks, s...  18.6 us
    ppermute x3, starting transfers between devices, shifts(): left = lax.ppermute(cells, 'ent', [(i, i + 1) for i in range(ends - 1)])  13.2 us
    unnamed x32, local copies, waits for them, and re-layouts  11.9 us
    ppermute x3, starting transfers between devices, shifts(): right = lax.ppermute(cells, 'ent', [(i + 1, i) for i in range(ends - 1)])  3.88 us
  transfers between devices with their start and end apart: 16, of which 6 were waited for; matrix products, arithmetic and copies ran while one was open for 10% of the time, Pallas kernels for 23%

profile of v1, /device:TPU:0, one launch (start us, length us, event | category | flops | bytes accessed | tf_op | source)
XLA Modules:
  0.0 191.9 jit_solution(6573700742683288915)
XLA Ops:
  0.6 4.9 %collective-permute-start = (bf16[64,1024]{1,0:T(8,128)(2,1)}, bf16[64,1024]{1,0:T(8,128)(2,1)S(1)}, u32[]{:S(2)}, u32[]{:S(2)}) collective-permute-start(bf16[64,1024]{1,0:T(8,128)(2,1)} %refs_0_.1), channel_id=1, source_target_pairs={{0,4},{4,8},{8,12},{12,16},{16,20},{20,24},{24,28},{1,5},{5,9},{9,... | collective-permute-start | bytes 393224 | tf_op jit(solution)/shard_map/ppermute | solution.py:410
  14.8 2.1 %copy.35.rel_table = bf16[3,822,64]{2,1,0:T(8,128)(2,1)} copy(bf16[3,822,64]{1,2,0:T(8,128)(2,1)} %param.25) | data formatting | bytes 631296 | tf_op args[4]
  16.8 18.6 %prep.1 = (bf16[128,128,128]{2,1,0:T(8,128)(2,1)}, f32[3,136,256]{2,1,0:T(8,128)}, f32[8,256]{1,0:T(8,128)}, s32[8,256]{1,0:T(8,128)}, s32[593]{0:T(1024)}) custom-call(s32[80,2]{1,0:T(8,128)} %copy.31.reg_blocks, s32[24,2]{1,0:T(8,128)} %copy.32.hin_blocks, s32[24,2]{1,0:T(8,128)} %copy.33.hout_blocks, s32[80]{0:T(128)} %reg_rel.1, s32[24]{0:T(128)} %hin_rel.1, ...), custom_call_target="tpu_custom_call" | custom-call | bytes 12582912 | tf_op jit(solution)/shard_map/prep/pallas_call | solution.py:364
  40.3 8.2 %own.3 = (bf16[1024,256]{1,0:T(8,128)(2,1)}, f32[1024,256]{1,0:T(8,128)}, f32[128,256]{1,0:T(8,128)}) custom-call(s32[593]{0:T(1024)} %get-tuple-element.18.order, bf16[128,128,128]{2,1,0:T(8,128)(2,1)} %get-tuple-element.19.turned, f32[136,256]{1,0:T(8,128)} %get-tuple-element.34.rel_row, bf16[64,1024]{1,0:T(8,128)(2,1)} %refs_0_.1, ...), custom_call_target="tpu_custom_call" | custom-call | flops 536870912 | bytes 4194304 | tf_op jit(solution)/shard_map/own/pallas_call | solution.py:422
  49.3 8.4 %close.3.refs_0_.own = bf16[1024,256]{1,0:T(8,128)(2,1)} custom-call(s32[593]{0:T(1024)} %get-tuple-element.18.order, bf16[128,128,128]{2,1,0:T(8,128)(2,1)} %get-tuple-element.19.turned, f32[136,256]{1,0:T(8,128)} %get-tuple-element.34.rel_row, bf16[1024,256]{1,0:T(8,128)(2,1)} %get-tuple-element.23.own, f32[1024,256]{1,0:T(8,128)} %get-tuple-element.24.total_in, ...), custom_call_target="tpu_custom_call" | custom-call | flops 1073741824 | bytes 8388608 | tf_op jit(solution)/shard_map/close/pallas_call | solution.py:422
  57.6 5.6 %collective-permute-start.2 = (bf16[1024,256]{1,0:T(8,128)(2,1)}, bf16[1024,256]{1,0:T(8,128)(2,1)S(1)}, u32[]{:S(2)}, u32[]{:S(2)}) collective-permute-start(bf16[1024,256]{1,0:T(8,128)(2,1)} %close.3.refs_0_.own), channel_id=1, source_target_pairs={{0,4},{4,8},{8,12},{12,16},{16,20},{20,24},{24,28},{1,5},{5,9},{9,... | collective-permute-start | bytes 1572872 | tf_op jit(solution)/shard_map/ppermute | solution.py:410
  64.5 3.1 %collective-permute-start.4 = (f32[128,256]{1,0:T(8,128)S(1)}, f32[128,256]{1,0:T(8,128)S(1)}, u32[]{:S(2)}, u32[]{:S(2)}) collective-permute-start(f32[128,256]{1,0:T(8,128)S(1)} %copy-done.7), channel_id=1, source_target_pairs={{0,4},{4,0},{8,12},{12,8},{16,20},{20,16},{24,28},{28,24},{1,5},{5... | collective-permute-start | bytes 393224 | tf_op jit(solution)/shard_map/ppermute | solution.py:417
  67.7 20.4 %collective-permute-done.4 = f32[128,256]{1,0:T(8,128)S(1)} collective-permute-done((f32[128,256]{1,0:T(8,128)S(1)}, f32[128,256]{1,0:T(8,128)S(1)}, u32[]{:S(2)}, u32[]{:S(2)}) %collective-permute-start.4) | collective-permute-done | bytes 131104 | tf_op jit(solution)/shard_map/ppermute | solution.py:417
  88.1 4.4 %collective-permute-start.5 = (f32[128,256]{1,0:T(8,128)S(1)}, f32[128,256]{1,0:T(8,128)S(1)}, u32[]{:S(2)}, u32[]{:S(2)}) collective-permute-start(f32[128,256]{1,0:T(8,128)S(1)} %add.42), channel_id=1, source_target_pairs={{0,8},{4,12},{8,0},{12,4},{16,24},{20,28},{24,16},{28,20},{1,9},{5... | collective-permute-start | bytes 393224 | tf_op jit(solution)/shard_map/ppermute | solution.py:417
  92.5 3.7 %collective-permute-done.5 = f32[128,256]{1,0:T(8,128)S(1)} collective-permute-done((f32[128,256]{1,0:T(8,128)S(1)}, f32[128,256]{1,0:T(8,128)S(1)}, u32[]{:S(2)}, u32[]{:S(2)}) %collective-permute-start.5) | collective-permute-done | bytes 131104 | tf_op jit(solution)/shard_map/ppermute | solution.py:417
  96.2 2.8 %collective-permute-start.6 = (f32[128,256]{1,0:T(8,128)S(1)}, f32[128,256]{1,0:T(8,128)S(1)}, u32[]{:S(2)}, u32[]{:S(2)}) collective-permute-start(f32[128,256]{1,0:T(8,128)S(1)} %add.43), channel_id=1, source_target_pairs={{0,16},{4,20},{8,24},{12,28},{16,0},{20,4},{24,8},{28,12},{1,17},{... | collective-permute-start | bytes 393224 | tf_op jit(solution)/shard_map/ppermute | solution.py:417
  99.0 7.8 %own.4 = (f32[1024,256]{1,0:T(8,128)}, f32[128,256]{1,0:T(8,128)}) custom-call(s32[593]{0:T(1024)} %get-tuple-element.18.order, bf16[128,128,128]{2,1,0:T(8,128)(2,1)} %get-tuple-element.19.turned, f32[136,256]{1,0:T(8,128)} %get-tuple-element.35.rel_row, bf16[1024,256]{1,0:T(8,128)(2,1)} %close.3.refs_0_.own), custom_call_target="tpu_custom_call" | custom-call | flops 536870912 | bytes 4194304 | tf_op jit(solution)/shard_map/own/pallas_call | solution.py:422
  108.5 10.2 %close.4 = (bf16[1024,256]{1,0:T(8,128)(2,1)}, bf16[128,256]{1,0:T(8,128)(2,1)}) custom-call(s32[593]{0:T(1024)} %get-tuple-element.18.order, bf16[128,128,128]{2,1,0:T(8,128)(2,1)} %get-tuple-element.19.turned, f32[136,256]{1,0:T(8,128)} %get-tuple-element.35.rel_row, bf16[1024,256]{1,0:T(8,128)(2,1)} %close.3.refs_0_.own, ...), custom_call_target="tpu_custom_call" | custom-call | flops 1073741824 | bytes 8388608 | tf_op jit(solution)/shard_map/close/pallas_call | solution.py:422
  118.7 2.7 %collective-permute-start.7 = (bf16[1024,256]{1,0:T(8,128)(2,1)}, bf16[1024,256]{1,0:T(8,128)(2,1)S(1)}, u32[]{:S(2)}, u32[]{:S(2)}) collective-permute-start(bf16[1024,256]{1,0:T(8,128)(2,1)} %get-tuple-element.27.refs_0_.own), channel_id=1, source_target_pairs={{0,4},{4,8},{8,12},{12,16},{16,20},{20,24},{24,28},{1,5},{5,9},{9,... | collective-permute-start | bytes 1572872 | tf_op jit(solution)/shard_map/ppermute | solution.py:410
  122.7 3.7 %collective-permute-start.9 = (f32[128,256]{1,0:T(8,128)S(1)}, f32[128,256]{1,0:T(8,128)S(1)}, u32[]{:S(2)}, u32[]{:S(2)}) collective-permute-start(f32[128,256]{1,0:T(8,128)S(1)} %copy-done.6), channel_id=1, source_target_pairs={{0,4},{4,0},{8,12},{12,8},{16,20},{20,16},{24,28},{28,24},{1,5},{5... | collective-permute-start | bytes 393224 | tf_op jit(solution)/shard_map/ppermute | solution.py:417
  126.4 7.8 %own.5 = (f32[1024,256]{1,0:T(8,128)}, f32[128,256]{1,0:T(8,128)}) custom-call(s32[593]{0:T(1024)} %get-tuple-element.18.order, bf16[128,128,128]{2,1,0:T(8,128)(2,1)} %get-tuple-element.19.turned, f32[136,256]{1,0:T(8,128)} %get-tuple-element.36.rel_row, bf16[1024,256]{1,0:T(8,128)(2,1)} %get-tuple-element.27.refs_0_.own), custom_call_target="tpu_custom_call" | custom-call | flops 536870912 | bytes 4194304 | tf_op jit(solution)/shard_map/own/pallas_call | solution.py:422
  134.2 12.9 %collective-permute-done.9 = f32[128,256]{1,0:T(8,128)S(1)} collective-permute-done((f32[128,256]{1,0:T(8,128)S(1)}, f32[128,256]{1,0:T(8,128)S(1)}, u32[]{:S(2)}, u32[]{:S(2)}) %collective-permute-start.9) | collective-permute-done | bytes 131104 | tf_op jit(solution)/shard_map/ppermute | solution.py:417
  147.1 3.9 %collective-permute-start.10 = (f32[128,256]{1,0:T(8,128)S(1)}, f32[128,256]{1,0:T(8,128)S(1)}, u32[]{:S(2)}, u32[]{:S(2)}) collective-permute-start(f32[128,256]{1,0:T(8,128)S(1)} %add.45), channel_id=1, source_target_pairs={{0,8},{4,12},{8,0},{12,4},{16,24},{20,28},{24,16},{28,20},{1,9},{5... | collective-permute-start | bytes 393224 | tf_op jit(solution)/shard_map/ppermute | solution.py:417
  151.9 2.7 %collective-permute-start.13 = (f32[128,256]{1,0:T(8,128)S(1)}, f32[128,256]{1,0:T(8,128)S(1)}, u32[]{:S(2)}, u32[]{:S(2)}) collective-permute-start(f32[128,256]{1,0:T(8,128)S(1)} %add.48), channel_id=1, source_target_pairs={{0,8},{4,12},{8,0},{12,4},{16,24},{20,28},{24,16},{28,20},{1,9},{5... | collective-permute-start | bytes 393224 | tf_op jit(solution)/shard_map/ppermute | solution.py:417
  156.4 3.1 %collective-permute-done.13 = f32[128,256]{1,0:T(8,128)S(1)} collective-permute-done((f32[128,256]{1,0:T(8,128)S(1)}, f32[128,256]{1,0:T(8,128)S(1)}, u32[]{:S(2)}, u32[]{:S(2)}) %collective-permute-start.13) | collective-permute-done | bytes 131104 | tf_op jit(solution)/shard_map/ppermute | solution.py:417
  161.0 6.3 %collective-permute-done.11 = f32[128,256]{1,0:T(8,128)S(1)} collective-permute-done((f32[128,256]{1,0:T(8,128)S(1)}, f32[128,256]{1,0:T(8,128)S(1)}, u32[]{:S(2)}, u32[]{:S(2)}) %collective-permute-start.11) | collective-permute-done | bytes 131104 | tf_op jit(solution)/shard_map/ppermute | solution.py:417
  170.8 11.9 %close.5 = (f32[8,1024]{1,0:T(8,128)}, bf16[128,256]{1,0:T(8,128)(2,1)}) custom-call(s32[593]{0:T(1024)} %get-tuple-element.18.order, bf16[128,128,128]{2,1,0:T(8,128)(2,1)} %get-tuple-element.19.turned, f32[136,256]{1,0:T(8,128)} %get-tuple-element.36.rel_row, bf16[1024,256]{1,0:T(8,128)(2,1)} %get-tuple-element.27.refs_0_.own, ...), custom_call_target="tpu_custom_call" | custom-call | flops 1073741824 | bytes 8388608 | tf_op jit(solution)/shard_map/close/pallas_call | solution.py:422
  184.1 3.2 %all-to-all-start = ((f32[4,4,256]{2,0,1:T(4,128)}), f32[4,4,256]{2,0,1:T(4,128)S(1)}, u32[]{:S(2)}, u32[]{:S(2)}) async-start(f32[4,4,256]{2,0,1:T(4,128)} %bitcast.6), calls=%async_computation | async-start | bytes 32768 | tf_op jit(solution)/shard_map/all_to_all | solution.py:479
  187.4 2.6 %hubs.1 = f32[8,128]{1,0:T(8,128)} custom-call(f32[128,256]{1,0:T(8,128)} %add.50.hub_sum, bf16[128,256]{1,0:T(8,128)(2,1)} %get-tuple-element.33.hub_old, f32[8,256]{1,0:T(8,128)} %get-tuple-element.21.refs_1_.lane_rows, f32[10,256]{1,0:T(8,128)} %tile.9.params, bf16[4,256,256]{2,1,0:T(8,128)(2,1)} %broadcast_select_fusion.weights), custom_call_target="tpu_custom_call" | custom-call | tf_op jit(solution)/shard_map/hubs/pallas_call | solution.py:422
  (72 shorter events, 30.0 us)
Async XLA Ops:
  0.6 47.9 %collective-permute-start = (bf16[64,1024]{1,0:T(8,128)(2,1)}, bf16[64,1024]{1,0:T(8,128)(2,1)S(1)}, u32[]{:S(2)}, u32[]{:S(2)}) collective-permute-start(bf16[64,1024]{1,0:T(8,128)(2,1)} %refs_0_.1), channel_id=1, source_target_pairs={{0,4},{4,8},{8,12},{12,16},{16,20},{20,24},{24,28},{1,5},{5,9},{9,... | collective-permute-start | bytes 393224 | tf_op jit(solution)/shard_map/ppermute | solution.py:410
  5.5 43.1 %collective-permute-start.1 = (bf16[64,1024]{1,0:T(8,128)(2,1)}, bf16[64,1024]{1,0:T(8,128)(2,1)S(1)}, u32[]{:S(2)}, u32[]{:S(2)}) collective-permute-start(bf16[64,1024]{1,0:T(8,128)(2,1)} %refs_0_.1), channel_id=1, source_target_pairs={{4,0},{8,4},{12,8},{16,12},{20,16},{24,20},{28,24},{5,1},{9,5},{13... | collective-permute-start | bytes 393224 | tf_op jit(solution)/shard_map/ppermute | solution.py:411
  16.8 20.7 %copy-start.8 = (bf16[3,64,64]{2,1,0:T(8,128)(2,1)S(1)}, bf16[3,64,64]{2,1,0:T(8,128)(2,1)}, u32[]{:S(2)}) copy-start(bf16[3,64,64]{2,1,0:T(8,128)(2,1)} %param.26) | copy-start | bytes 73732
  35.5 4.1 %copy-start.9 = (f32[3,64]{1,0:T(4,128)S(1)}, f32[3,64]{1,0:T(4,128)}, u32[]{:S(2)}) copy-start(f32[3,64]{1,0:T(4,128)} %param.29) | copy-start | bytes 2308
  35.5 4.1 %copy-start.10 = (f32[3,64]{1,0:T(4,128)S(1)}, f32[3,64]{1,0:T(4,128)}, u32[]{:S(2)}) copy-start(f32[3,64]{1,0:T(4,128)} %param.28) | copy-start | bytes 2308
  35.5 4.1 %copy-start.11 = (f32[3,64]{1,0:T(4,128)S(1)}, f32[3,64]{1,0:T(4,128)}, u32[]{:S(2)}) copy-start(f32[3,64]{1,0:T(4,128)} %param.27) | copy-start | bytes 2308
  35.5 4.1 %copy-start.12 = (f32[64]{0:T(128)S(1)}, f32[64]{0:T(128)}, u32[]{:S(2)}) copy-start(f32[64]{0:T(128)} %param.41) | copy-start | bytes 772
  48.6 16.0 %copy-start.7 = (f32[128,256]{1,0:T(8,128)S(1)}, f32[128,256]{1,0:T(8,128)}, u32[]{:S(2)}) copy-start(f32[128,256]{1,0:T(8,128)} %get-tuple-element.26) | copy-start | bytes 393220
  57.6 49.8 %collective-permute-start.2 = (bf16[1024,256]{1,0:T(8,128)(2,1)}, bf16[1024,256]{1,0:T(8,128)(2,1)S(1)}, u32[]{:S(2)}, u32[]{:S(2)}) collective-permute-start(bf16[1024,256]{1,0:T(8,128)(2,1)} %close.3.refs_0_.own), channel_id=1, source_target_pairs={{0,4},{4,8},{8,12},{12,16},{16,20},{20,24},{24,28},{1,5},{5,9},{9,... | collective-permute-start | bytes 1572872 | tf_op jit(solution)/shard_map/ppermute | solution.py:410
  63.2 44.3 %collective-permute-start.3 = (bf16[1024,256]{1,0:T(8,128)(2,1)}, bf16[1024,256]{1,0:T(8,128)(2,1)S(1)}, u32[]{:S(2)}, u32[]{:S(2)}) collective-permute-start(bf16[1024,256]{1,0:T(8,128)(2,1)} %close.3.refs_0_.own), channel_id=1, source_target_pairs={{4,0},{8,4},{12,8},{16,12},{20,16},{24,20},{28,24},{5,1},{9,5},{13... | collective-permute-start | bytes 1572872 | tf_op jit(solution)/shard_map/ppermute | solution.py:411
  64.5 23.5 %collective-permute-start.4 = (f32[128,256]{1,0:T(8,128)S(1)}, f32[128,256]{1,0:T(8,128)S(1)}, u32[]{:S(2)}, u32[]{:S(2)}) collective-permute-start(f32[128,256]{1,0:T(8,128)S(1)} %copy-done.7), channel_id=1, source_target_pairs={{0,4},{4,0},{8,12},{12,8},{16,20},{20,16},{24,28},{28,24},{1,5},{5... | collective-permute-start | bytes 393224 | tf_op jit(solution)/shard_map/ppermute | solution.py:417
  88.1 8.1 %collective-permute-start.5 = (f32[128,256]{1,0:T(8,128)S(1)}, f32[128,256]{1,0:T(8,128)S(1)}, u32[]{:S(2)}, u32[]{:S(2)}) collective-permute-start(f32[128,256]{1,0:T(8,128)S(1)} %add.42), channel_id=1, source_target_pairs={{0,8},{4,12},{8,0},{12,4},{16,24},{20,28},{24,16},{28,20},{1,9},{5... | collective-permute-start | bytes 393224 | tf_op jit(solution)/shard_map/ppermute | solution.py:417
  96.2 10.6 %collective-permute-start.6 = (f32[128,256]{1,0:T(8,128)S(1)}, f32[128,256]{1,0:T(8,128)S(1)}, u32[]{:S(2)}, u32[]{:S(2)}) collective-permute-start(f32[128,256]{1,0:T(8,128)S(1)} %add.43), channel_id=1, source_target_pairs={{0,16},{4,20},{8,24},{12,28},{16,0},{20,4},{24,8},{28,12},{1,17},{... | collective-permute-start | bytes 393224 | tf_op jit(solution)/shard_map/ppermute | solution.py:417
  106.8 15.9 %copy-start.6 = (f32[128,256]{1,0:T(8,128)S(1)}, f32[128,256]{1,0:T(8,128)}, u32[]{:S(2)}) copy-start(f32[128,256]{1,0:T(8,128)} %get-tuple-element.29) | copy-start | bytes 393220
  107.5 1.0 copy-start.3
  118.7 51.1 %collective-permute-start.7 = (bf16[1024,256]{1,0:T(8,128)(2,1)}, bf16[1024,256]{1,0:T(8,128)(2,1)S(1)}, u32[]{:S(2)}, u32[]{:S(2)}) collective-permute-start(bf16[1024,256]{1,0:T(8,128)(2,1)} %get-tuple-element.27.refs_0_.own), channel_id=1, source_target_pairs={{0,4},{4,8},{8,12},{12,16},{16,20},{20,24},{24,28},{1,5},{5,9},{9,... | collective-permute-start | bytes 1572872 | tf_op jit(solution)/shard_map/ppermute | solution.py:410
  121.4 48.4 %collective-permute-start.8 = (bf16[1024,256]{1,0:T(8,128)(2,1)}, bf16[1024,256]{1,0:T(8,128)(2,1)S(1)}, u32[]{:S(2)}, u32[]{:S(2)}) collective-permute-start(bf16[1024,256]{1,0:T(8,128)(2,1)} %get-tuple-element.27.refs_0_.own), channel_id=1, source_target_pairs={{4,0},{8,4},{12,8},{16,12},{20,16},{24,20},{28,24},{5,1},{9,5},{13... | collective-permute-start | bytes 1572872 | tf_op jit(solution)/shard_map/ppermute | solution.py:411
  122.7 24.4 %collective-permute-start.9 = (f32[128,256]{1,0:T(8,128)S(1)}, f32[128,256]{1,0:T(8,128)S(1)}, u32[]{:S(2)}, u32[]{:S(2)}) collective-permute-start(f32[128,256]{1,0:T(8,128)S(1)} %copy-done.6), channel_id=1, source_target_pairs={{0,4},{4,0},{8,12},{12,8},{16,20},{20,16},{24,28},{28,24},{1,5},{5... | collective-permute-start | bytes 393224 | tf_op jit(solution)/shard_map/ppermute | solution.py:417
  134.2 16.8 %collective-permute-start.12 = (f32[128,256]{1,0:T(8,128)}, f32[128,256]{1,0:T(8,128)S(1)}, u32[]{:S(2)}, u32[]{:S(2)}) collective-permute-start(f32[128,256]{1,0:T(8,128)} %get-tuple-element.32), channel_id=1, source_target_pairs={{0,4},{4,0},{8,12},{12,8},{16,20},{20,16},{24,28},{28,24},{1,5},{5... | collective-permute-start | bytes 393224 | tf_op jit(solution)/shard_map/ppermute | solution.py:417
  147.1 7.5 %collective-permute-start.10 = (f32[128,256]{1,0:T(8,128)S(1)}, f32[128,256]{1,0:T(8,128)S(1)}, u32[]{:S(2)}, u32[]{:S(2)}) collective-permute-start(f32[128,256]{1,0:T(8,128)S(1)} %add.45), channel_id=1, source_target_pairs={{0,8},{4,12},{8,0},{12,4},{16,24},{20,28},{24,16},{28,20},{1,9},{5... | collective-permute-start | bytes 393224 | tf_op jit(solution)/shard_map/ppermute | solution.py:417
  151.9 7.6 %collective-permute-start.13 = (f32[128,256]{1,0:T(8,128)S(1)}, f32[128,256]{1,0:T(8,128)S(1)}, u32[]{:S(2)}, u32[]{:S(2)}) collective-permute-start(f32[128,256]{1,0:T(8,128)S(1)} %add.48), channel_id=1, source_target_pairs={{0,8},{4,12},{8,0},{12,4},{16,24},{20,28},{24,16},{28,20},{1,9},{5... | collective-permute-start | bytes 393224 | tf_op jit(solution)/shard_map/ppermute | solution.py:417
  154.6 12.8 %collective-permute-start.11 = (f32[128,256]{1,0:T(8,128)S(1)}, f32[128,256]{1,0:T(8,128)S(1)}, u32[]{:S(2)}, u32[]{:S(2)}) collective-permute-start(f32[128,256]{1,0:T(8,128)S(1)} %add.46), channel_id=1, source_target_pairs={{0,16},{4,20},{8,24},{12,28},{16,0},{20,4},{24,8},{28,12},{1,17},{... | collective-permute-start | bytes 393224 | tf_op jit(solution)/shard_map/ppermute | solution.py:417
  159.5 9.7 %collective-permute-start.14 = (f32[128,256]{1,0:T(8,128)S(1)}, f32[128,256]{1,0:T(8,128)S(1)}, u32[]{:S(2)}, u32[]{:S(2)}) collective-permute-start(f32[128,256]{1,0:T(8,128)S(1)} %add.49), channel_id=1, source_target_pairs={{0,16},{4,20},{8,24},{12,28},{16,0},{20,4},{24,8},{28,12},{1,17},{... | collective-permute-start | bytes 393224 | tf_op jit(solution)/shard_map/ppermute | solution.py:417
  184.1 7.2 %all-to-all-start = ((f32[4,4,256]{2,0,1:T(4,128)}), f32[4,4,256]{2,0,1:T(4,128)S(1)}, u32[]{:S(2)}, u32[]{:S(2)}) async-start(f32[4,4,256]{2,0,1:T(4,128)} %bitcast.6), calls=%async_computation | async-start | bytes 32768 | tf_op jit(solution)/shard_map/all_to_all | solution.py:479
  (5 other events, 3.8 us)

commit v2 on v1

v2 whole, which is shorter than its diff:
```python
import functools
import math

import jax
import jax.numpy as jnp
from jax import lax
from jax.experimental import pallas as pl
from jax.experimental.pallas import tpu as pltpu
from jax.sharding import PartitionSpec as P

HUB_DEV = 16
JOIN = 2
F32 = jnp.float32
BF16 = jnp.bfloat16
SMEM = pl.BlockSpec(memory_space=pltpu.SMEM)
VMEM = pl.BlockSpec(memory_space=pltpu.VMEM)
LEFT, OWN, RIGHT, HOUT, HIN = range(5)


class Plan:
    def __init__(self, counts, blocks, hub_blocks):
        reg, hin, hout = counts
        self.tiles = reg + hin + hout
        self.keys = [blocks, blocks, blocks, blocks, hub_blocks]
        mean = [reg / (3 * blocks)] * 3 + [hout / blocks, hin / hub_blocks]
        most = [reg] * 3 + [hout, hin]
        self.slots = [
            min(m + m % 2, 2 * math.ceil((a + 1.2 * math.sqrt(a)) / 2)) for a, m in zip(mean, most)
        ]
        self.first_key = [sum(self.keys[:s]) for s in range(5)]
        place = 16
        self.main = []
        for side in range(5):
            self.main.append(place)
            place += self.keys[side] * self.slots[side]
        self.target = []
        self.more = []
        for side in range(5):
            room = most[side] // JOIN + self.keys[side]
            self.target.append(place)
            self.more.append(place + room)
            place += room * (1 + JOIN)
        self.size = place


def spreader(width, lanes, transposed=False):
    shape = (lanes, width) if transposed else (width, lanes)
    row = lax.broadcasted_iota(jnp.int32, shape, 0)
    column = lax.broadcasted_iota(jnp.int32, shape, 1)
    hit = lax.rem(row, width) == column if transposed else lax.rem(column, width) == row
    return hit.astype(F32).astype(BF16)


def contract_last(a, b):
    return lax.dot_general(a, b, (((1,), (1,)), ((), ())), preferred_element_type=F32)


def prep_kernel(
    plan, blocks, splits, layers,
    reg_blocks, hin_blocks, hout_blocks, query_head, query_rel, reg_rel, hin_rel, hout_rel,
    query_table, rel_table, read_weight, read_bias, read_out, layer_weight, layer_bias, norm_gain,
    norm_shift, reg_mask, hin_mask, hout_mask,
    turned, rel_rows, lane_rows, lane_heads, weights, order, q_rows, count_of, chunk_of, used,
):
    step = pl.program_id(0)
    relations = query_table.shape[1]
    width = query_table.shape[0]
    lanes = lane_rows.shape[1]
    q_local = lanes // width
    block = turned.shape[1]

    @pl.when(step == 0)
    def _():
        first_block = lax.axis_index("ent") * blocks
        query_first = lax.axis_index("qry") * q_local
        for key in range(sum(plan.keys)):
            count_of[key] = 0
        for side in range(5):
            used[side] = 0
        empty = plan.tiles

        def clear(i, _):
            order[i] = empty
            return 0

        lax.fori_loop(plan.main[0], plan.target[0], clear, 0, unroll=8)

        def note(tile, side, local, source, slots, main, target, more, first_key):
            key = first_key + local
            seen = count_of[key]
            word = tile + source * 4096
            count_of[key] = seen + 1

            @pl.when(seen < slots)
            def _():
                order[main + local * slots + seen] = word

            @pl.when(seen >= slots)
            def _():
                over = seen - slots
                within = lax.rem(over, JOIN)

                @pl.when(within == 0)
                def _():
                    fresh = used[side]
                    used[side] = fresh + 1
                    chunk_of[key] = fresh
                    order[target + fresh] = local
                    for u in range(1, JOIN):
                        order[more + fresh * JOIN + u] = empty

                order[more + chunk_of[key] * JOIN + within] = word

        def pick(side, table):
            return jnp.where(side == 0, table[0], jnp.where(side == 1, table[1], table[2]))

        def note_reg(t, _):
            place = reg_blocks[1, t] - first_block + blocks
            side = lax.div(place, blocks)
            note(
                t, side, reg_blocks[0, t] - first_block, place - side * blocks, plan.slots[0],
                plan.main[0] + side * (plan.main[1] - plan.main[0]),
                plan.target[0] + side * (plan.target[1] - plan.target[0]),
                plan.more[0] + side * (plan.more[1] - plan.more[0]),
                side * blocks,
            )
            return 0

        def note_hin(t, _):
            note(
                reg_blocks.shape[1] + t, HIN, hin_blocks[0, t], hin_blocks[1, t] - first_block,
                plan.slots[HIN], plan.main[HIN], plan.target[HIN], plan.more[HIN], plan.first_key[HIN],
            )
            return 0

        def note_hout(t, _):
            note(
                reg_blocks.shape[1] + hin_blocks.shape[1] + t, HOUT, hout_blocks[0, t] - first_block,
                hout_blocks[1, t], plan.slots[HOUT], plan.main[HOUT], plan.target[HOUT],
                plan.more[HOUT], plan.first_key[HOUT],
            )
            return 0

        lax.fori_loop(0, reg_blocks.shape[1], note_reg, 0)
        lax.fori_loop(0, hin_blocks.shape[1], note_hin, 0)
        lax.fori_loop(0, hout_blocks.shape[1], note_hout, 0)
        for side in range(5):
            order[side] = used[side]

        spread = spreader(width, lanes)
        spread_back = spreader(width, lanes, True)

        def picked(table, ids):
            row = lax.broadcasted_iota(jnp.int32, (relations, ids.shape[1]), 0)
            hit = (row == ids[...]).astype(F32).astype(BF16)
            return jnp.transpose(jnp.dot(table, hit, preferred_element_type=F32))

        rel_rows[...] = jnp.zeros_like(rel_rows)
        base = 0
        for ids in (reg_rel, hin_rel, hout_rel):
            count = ids.shape[1]
            for layer in range(layers):
                rows = picked(rel_table[layer], ids)
                rel_rows[layer, base : base + count, :] = jnp.dot(
                    rows.astype(BF16), spread, preferred_element_type=F32
                )
            base += count

        q_rows[...] = picked(query_table[...], query_rel)
        q_of_lane = lax.div(lax.broadcasted_iota(jnp.int32, (1, lanes), 1), width)
        wide = jnp.dot(q_rows[...].astype(BF16), spread, preferred_element_type=F32)
        parts = contract_last(q_rows[...].astype(BF16), read_weight[:, width:]) + read_bias[...]

        def wide_rows(rows):
            return jnp.dot(rows, spread.astype(F32), precision=lax.Precision.HIGHEST)

        wide_parts = wide_rows(parts)
        query_at = lax.broadcasted_iota(jnp.int32, wide.shape, 0) - query_first
        mine = query_at == q_of_lane
        lane_rows[...] = jnp.zeros_like(lane_rows)
        lane_rows[0:1, :] = jnp.sum(jnp.where(mine, wide, 0.0), axis=0, keepdims=True)
        lane_rows[1:2, :] = jnp.sum(jnp.where(mine, wide_parts, 0.0), axis=0, keepdims=True)
        lane_rows[2:3, :] = wide_rows(read_out[...])
        for at, rows in ((3, layer_bias), (3 + layers, norm_gain), (3 + 2 * layers, norm_shift)):
            lane_rows[at : at + layers, :] = wide_rows(rows[...])
        lane_head = jnp.zeros((1, lanes), jnp.int32)
        for q in range(q_local):
            lane_head = jnp.where(q_of_lane == q, query_head[query_first + q], lane_head)
        lane_heads[...] = jnp.broadcast_to(lane_head, lane_heads.shape)

        same = lax.div(lax.broadcasted_iota(jnp.int32, (lanes, lanes), 0), width) == lax.div(
            lax.broadcasted_iota(jnp.int32, (lanes, lanes), 1), width
        )
        for layer in range(layers + 1):
            if layer < layers:
                tall = jnp.dot(spread_back, layer_weight[layer], preferred_element_type=F32)
            else:
                tall = contract_last(spread_back, read_weight[:, :width])
            full = jnp.dot(tall.astype(BF16), spread, preferred_element_type=F32)
            weights[layer] = jnp.where(same, full, 0.0).astype(BF16)
        weights[layers + 1] = jnp.where(same, 1.0 / width, 0.0).astype(BF16)

    def turn(mask):
        eye = lax.broadcasted_iota(jnp.int32, (block, block), 0) == lax.broadcasted_iota(
            jnp.int32, (block, block), 1
        )
        eye = eye.astype(F32).astype(BF16)
        for t in range(mask.shape[0]):
            turned[t] = contract_last(eye, mask[t].astype(F32).astype(BF16)).astype(BF16)

    pl.when(step < splits[0])(lambda: turn(reg_mask))
    pl.when((step >= splits[0]) & (step < splits[1]))(lambda: turn(hin_mask))
    pl.when(step >= splits[1])(lambda: turn(hout_mask))


def split_dot(values, matrix):
    high = values.astype(BF16)
    low = (values - high.astype(F32)).astype(BF16)
    return jnp.dot(high, matrix, preferred_element_type=F32) + jnp.dot(
        low, matrix, preferred_element_type=F32
    )


def slot_product(plan, layer, order, turned, rel_rows, places):
    block = turned.shape[1]
    lanes = rel_rows.shape[2]
    masks, values = [], []
    for place, source in places:
        word = order[place]
        tile = word & 4095
        start = pl.multiple_of((word >> 12) * block, block)
        row = jnp.broadcast_to(rel_rows[layer, pl.ds(tile, 1), :], (16, lanes)).astype(BF16)
        value = source[pl.ds(start, block), :].reshape(block // 16, 16, lanes)
        values.append((value * row[None]).reshape(block, lanes))
        masks.append(turned[jnp.where(tile == plan.tiles, 0, tile)])
    return jnp.dot(
        jnp.concatenate(masks, axis=1), jnp.concatenate(values, axis=0), preferred_element_type=F32
    )


def key_product(plan, layer, side_sources, key, order, turned, rel_rows):
    total = None
    for side, source in side_sources:
        slots = plan.slots[side]
        for start in range(0, slots, 6):
            places = [
                (plan.main[side] + key * slots + u, source) for u in range(start, min(start + 6, slots))
            ]
            product = slot_product(plan, layer, order, turned, rel_rows, places)
            total = product if total is None else total + product
    return total


def add_rest(plan, layer, side, source, order, turned, rel_rows, total):
    block = turned.shape[1]

    def chunk(c, _):
        places = [(plan.more[side] + c * JOIN + u, source) for u in range(JOIN)]
        place = pl.ds(pl.multiple_of(order[plan.target[side] + c] * block, block), block)
        total[place, :] += slot_product(plan, layer, order, turned, rel_rows, places)
        return 0

    lax.fori_loop(0, order[side], chunk, 0)


def normed_step(inputs, layer, layers, weights, lane_rows):
    means = weights[layers + 1]
    bias, gain, shift = (lane_rows[3 + layer + i * layers : 4 + layer + i * layers, :] for i in range(3))
    linear = jnp.dot(inputs, weights[layer], preferred_element_type=F32) + bias
    centered = linear - split_dot(linear, means)
    variance = split_dot(centered * centered, means)
    return jnp.maximum(centered * lax.rsqrt(variance + 1e-05) * gain + shift, 0.0)


def hit_lanes(rows, first, heads, values):
    place = first + lax.broadcasted_iota(jnp.int32, (rows, heads.shape[1]), 0)
    return jnp.where(place == heads, values, 0.0)


def first_states(feat, first, block, lane_rows, lane_heads, out):
    width, count = feat.shape
    columns = jnp.transpose(feat[...].astype(F32)).astype(BF16)
    spread = spreader(width, out.shape[1])
    for start in range(0, count, block):
        wide = jnp.dot(columns[start : start + block, :], spread, preferred_element_type=F32)
        hits = hit_lanes(block, first + start, lane_heads[0:1, :], lane_rows[0:1, :])
        out[start : start + block, :] = (wide + hits).astype(BF16)


def own_kernel(plan, layer, order, turned, rel_rows, *refs):
    block = turned.shape[1]
    if layer == 0:
        feat, lane_rows, lane_heads, states, total, hub_part = refs
        first = lax.axis_index("ent") * feat.shape[1]
        first_states(feat, first, block, lane_rows, lane_heads, states)
    else:
        states, total, hub_part = refs
    for side, out in ((HIN, hub_part), (OWN, total)):
        for key in range(plan.keys[side]):
            out[key * block : (key + 1) * block, :] = key_product(
                plan, layer, ((side, states),), key, order, turned, rel_rows
            )
        add_rest(plan, layer, side, states, order, turned, rel_rows, out)


def update_hubs(hub_sum, hub_old, layer, layers, weights, lane_rows):
    inputs = (hub_sum * lane_rows[0:1, :]).astype(BF16)
    grown = normed_step(inputs, layer, layers, weights, lane_rows)
    if hub_old is not None:
        grown = grown + hub_old.astype(F32)
    return grown.astype(BF16)


def hout_kernel(plan, layer, layers, order, turned, rel_rows, lane_rows, weights, total_in, hub_sum, *refs):
    block = turned.shape[1]
    if layer == 1:
        total, hub_new = refs
        hub_old = None
    else:
        old, total, hub_new = refs
        hub_old = old[...]
    hub_new[...] = update_hubs(hub_sum[...], hub_old, layer - 1, layers, weights, lane_rows)
    for key in range(plan.keys[HOUT]):
        place = slice(key * block, (key + 1) * block)
        total[place, :] = total_in[place, :] + key_product(
            plan, layer, ((HOUT, hub_new),), key, order, turned, rel_rows
        )
    add_rest(plan, layer, HOUT, hub_new, order, turned, rel_rows, total)


def score_rows(values, width, layers, weights, lane_rows):
    lanes = values.shape[1]
    row = lax.broadcasted_iota(jnp.int32, (8, lanes), 0)
    column = lax.broadcasted_iota(jnp.int32, (8, lanes), 1)
    picks = jnp.where(lax.div(column, width) == row, lane_rows[2:3, :], 0.0)
    features = jnp.dot(values, weights[layers], preferred_element_type=F32) + lane_rows[1:2, :]
    features = jnp.maximum(features, 0.0)
    high = features.astype(BF16)
    low = (features - high.astype(F32)).astype(BF16)
    pick_high = picks.astype(BF16)
    pick_low = (picks - pick_high.astype(F32)).astype(BF16)
    return contract_last(pick_high, high) + contract_last(pick_high, low) + contract_last(pick_low, high)


def close_kernel(plan, layer, layers, width, order, turned, rel_rows, lane_rows, lane_heads, weights, total_in, own, *refs):
    last = layer == layers - 1
    count = own.shape[0]
    block = turned.shape[1]
    first = lax.axis_index("ent") * count
    if layer == 0:
        left_feat, right_feat, out, total, left, right = refs
        first_states(left_feat, first - count, block, lane_rows, lane_heads, left)
        first_states(right_feat, first + count, block, lane_rows, lane_heads, right)
    else:
        left, right, out, total = refs
    total[...] = total_in[...]
    add_rest(plan, layer, LEFT, left, order, turned, rel_rows, total)
    add_rest(plan, layer, RIGHT, right, order, turned, rel_rows, total)
    lane_q = lane_rows[0:1, :]
    for key in range(plan.keys[LEFT]):
        place = slice(key * block, (key + 1) * block)
        sums = total[place, :] + key_product(
            plan, layer, ((LEFT, left), (RIGHT, right)), key, order, turned, rel_rows
        )
        hits = hit_lanes(block, first + key * block, lane_heads[0:1, :], lane_q)
        inputs = (sums * lane_q + hits).astype(BF16)
        grown = normed_step(inputs, layer, layers, weights, lane_rows)
        new = (grown + own[place, :].astype(F32)).astype(BF16)
        if last:
            out[:, place] = score_rows(new, width, layers, weights, lane_rows)[: out.shape[0]]
        else:
            out[place, :] = new


def hub_kernel(layers, width, lane_rows, weights, hub_sum, hub_old, out):
    mine = out.shape[1]
    place = pl.ds(pl.multiple_of(lax.axis_index("ent") * mine, mine), mine)
    new = update_hubs(hub_sum[place, :], hub_old[place, :], layers - 1, layers, weights, lane_rows)
    out[...] = score_rows(new, width, layers, weights, lane_rows)[: out.shape[0]]


def body(
    ent_feat, query_head, query_rel, query_table, rel_table, layer_weight, layer_bias, norm_gain,
    norm_shift, reg_blocks, reg_rel, reg_mask, hin_blocks, hin_rel, hin_mask, hout_blocks,
    hout_rel, hout_mask, read_weight, read_bias, read_out,
):
    ends = lax.axis_size("ent")
    layers = rel_table.shape[0]
    q_local = query_head.shape[0] // lax.axis_size("qry")
    width, ent_local = ent_feat.shape
    block = reg_mask.shape[1]
    blocks = ent_local // block
    hubs = HUB_DEV * ends
    lanes = q_local * width
    counts = [reg_mask.shape[0], hin_mask.shape[0], hout_mask.shape[0]]
    tiles = sum(counts)
    plan = Plan(counts, blocks, hubs // block)
    padded = tiles + 8
    queries = query_head.shape[0]

    group = 8
    while any(c % group for c in counts):
        group //= 2
    steps = [c // group for c in counts]
    splits = (steps[0], steps[0] + steps[1])

    def mask_spec(offset, length):
        return pl.BlockSpec(
            (group, block, block), lambda i: (jnp.clip(i - offset, 0, length - 1), 0, 0)
        )

    def whole(shape):
        return pl.BlockSpec(shape, lambda i: (0,) * len(shape))

    small = (
        query_rel[None, :], reg_rel[None, :], hin_rel[None, :], hout_rel[None, :],
        query_table.T, jnp.swapaxes(rel_table, 1, 2), read_weight.T, read_bias[None, :],
        read_out[None, :], layer_weight, layer_bias, norm_gain, norm_shift,
    )
    outs = (
        ((tiles, block, block), BF16), ((layers, padded, lanes), F32),
        ((8 * ((3 + 3 * layers + 7) // 8), lanes), F32), ((8, lanes), jnp.int32),
        ((layers + 2, lanes, lanes), BF16), ((plan.size,), jnp.int32),
    )
    keys = sum(plan.keys)
    turned, rel_rows, lane_rows, lane_heads, weights, order = pl.pallas_call(
        functools.partial(prep_kernel, plan, blocks, splits, layers),
        grid=(sum(steps),),
        in_specs=[SMEM] * 4
        + [whole(a.shape) for a in small]
        + [mask_spec(0, steps[0]), mask_spec(splits[0], steps[1]), mask_spec(splits[1], steps[2])],
        out_specs=[pl.BlockSpec((group, block, block), lambda i: (i, 0, 0))]
        + [whole(shape) for shape, _ in outs[1:5]]
        + [SMEM],
        out_shape=[jax.ShapeDtypeStruct(*o) for o in outs],
        scratch_shapes=[
            pltpu.VMEM((queries, width), F32),
            pltpu.SMEM((keys,), jnp.int32),
            pltpu.SMEM((keys,), jnp.int32),
            pltpu.SMEM((8,), jnp.int32),
        ],
        cost_estimate=pl.CostEstimate(
            flops=0, bytes_accessed=tiles * block * block * 6, transcendentals=0
        ),
        compiler_params=pltpu.CompilerParams(vmem_limit_bytes=16 << 20),
        name="prep",
    )(
        reg_blocks.T, hin_blocks.T, hout_blocks.T, query_head, *small, reg_mask, hin_mask, hout_mask,
    )

    def shifts(cells):
        left = lax.ppermute(cells, "ent", [(i, i + 1) for i in range(ends - 1)])
        right = lax.ppermute(cells, "ent", [(i + 1, i) for i in range(ends - 1)])
        return left, right

    def exchanged(part, strides):
        for stride in strides:
            part = part + lax.ppermute(part, "ent", [(i, i ^ stride) for i in range(ends)])
        return part

    far = [1 << i for i in range(1, ends.bit_length() - 1)]

    def call(kernel, name, operands, outs, scratch=(), tile_count=0, smem=1):
        return pl.pallas_call(
            kernel,
            in_specs=[SMEM] * smem + [VMEM] * (len(operands) - smem),
            out_specs=[VMEM] * len(outs),
            out_shape=outs,
            scratch_shapes=list(scratch),
            cost_estimate=pl.CostEstimate(
                flops=2 * tile_count * block * block * lanes,
                bytes_accessed=4 * tile_count * block * block,
                transcendentals=0,
            ),
            compiler_params=pltpu.CompilerParams(vmem_limit_bytes=16 << 20),
            name=name,
        )(*operands)

    state_shape = jax.ShapeDtypeStruct((ent_local, lanes), BF16)
    total_shape = jax.ShapeDtypeStruct((ent_local, lanes), F32)
    part_shape = jax.ShapeDtypeStruct((hubs, lanes), F32)
    hub_shape = jax.ShapeDtypeStruct((hubs, lanes), BF16)
    score_shape = jax.ShapeDtypeStruct((q_local, ent_local), F32)
    total_scratch = pltpu.VMEM((ent_local, lanes), F32)
    state_scratch = pltpu.VMEM((ent_local, lanes), BF16)
    tables = (order, turned, rel_rows)

    left, right = shifts(ent_feat)
    states, total, part = call(
        functools.partial(own_kernel, plan, 0), "own",
        tables + (ent_feat, lane_rows, lane_heads),
        (state_shape, total_shape, part_shape), (), tiles // 2,
    )
    hub_old = None
    hub_sum = None
    for layer in range(layers):
        last = layer == layers - 1
        if last:
            next_sum = exchanged(part, far + [1])
        elif layer == 0:
            part, left, right = lax.optimization_barrier((part, left, right))
            part = exchanged(part, [1])
        if layer > 0:
            old = () if layer == 1 else (hub_old,)
            total, hub_old = call(
                functools.partial(hout_kernel, plan, layer, layers), "hout",
                tables + (lane_rows, weights, total, hub_sum) + old, (total_shape, hub_shape), (), tiles // 4,
            )
            if not last:
                part, total = lax.optimization_barrier((part, total))
                part = exchanged(part, [1])
        (states,) = call(
            functools.partial(close_kernel, plan, layer, layers, width), "close",
            tables + (lane_rows, lane_heads, weights, total, states, left, right),
            (score_shape if last else state_shape,),
            (total_scratch,) + ((state_scratch, state_scratch) if layer == 0 else ()), tiles // 2,
        )
        if not last:
            states, part = lax.optimization_barrier((states, part))
            next_sum = exchanged(part, far)
        hub_sum = next_sum
        if not last:
            left, right = shifts(states)
            total, part = call(
                functools.partial(own_kernel, plan, layer + 1), "own",
                tables + (states,), (total_shape, part_shape), (), tiles // 2,
            )
    (hub_scores,) = call(
        functools.partial(hub_kernel, layers, width), "hubs",
        (lane_rows, weights, hub_sum, hub_old), (jax.ShapeDtypeStruct((q_local, HUB_DEV), F32),), smem=0,
    )
    scores = lax.all_to_all(states, "qry", split_axis=1, concat_axis=0, tiled=True)
    return scores, hub_scores


def solution(mesh):
    return jax.shard_map(
        body,
        mesh=mesh,
        in_specs=(
            P(None, "ent"), P(), P(), P(), P(), P(), P(), P(), P(),
            P("ent", None), P("ent"), P("ent", None, None),
            P("ent", None), P("ent"), P("ent", None, None),
            P("ent", None), P("ent"), P("ent", None, None),
            P(), P(), P(),
        ),
        out_specs=(P(None, ("ent", "qry")), P("qry", "ent")),
        check_vma=False,
    )
```

time: 193 us -> 139 us (0.72)
  Pallas kernels: 75.6 us -> 45.8 us
  waiting for transfers between devices: 47.5 us -> 38 us
  starting transfers between devices: 44.2 us -> 35.8 us
  other arithmetic: 4.02 us -> 0.16 us
    pallas_call x8 -> x10, Pallas kernels: 75.6 us -> 45.8 us  [the longest x9 31.7 us: call(): pl.pallas_call(kernel, in_specs=[SMEM] * smem + [VMEM] * (len(operands) -...]
    ppermute x9, waiting for transfers between devices: 47.5 us -> 35.5 us  [exchanged(): lax.ppermute(part, 'ent', [(i, i ^ stride) for i in range(ends)])]
    unnamed x32 -> x42, local copies, waits for them, and re-layouts: 11.9 us -> 17.3 us
    ppermute x3, starting transfers between devices: 13.2 us -> 8.45 us  [shifts(): left = lax.ppermute(cells, 'ent', [(i, i + 1) for i in range(ends - 1)])]
    ppermute x9, starting transfers between devices: 24 us -> 20.2 us  [exchanged(): lax.ppermute(part, 'ent', [(i, i ^ stride) for i in range(ends)])]
    add x9, other arithmetic: 3.04 us -> 0.16 us  [exchanged(): part + lax.ppermute(part, 'ent', [(i, i ^ stride) for i in range(ends)])]
    all_to_all x1, waiting for transfers between devices: 0.01 us -> 2.49 us  [body(): lax.all_to_all(states, 'qry', split_axis=1, concat_axis=0, tiled=True)]
  transfers between devices with their start and end apart: 16 -> 16, of which waited for: 6 -> 7; matrix products, arithmetic and copies ran while one was open for 10% -> 0% of each run, Pallas kernels for 23% -> 28%
where the time goes in v2:
time: 139 us
  Pallas kernels  45.8 us (33%)
  waiting for transfers between devices  38 us (27%)
  starting transfers between devices  35.8 us (26%)
  local copies, waits for them, and re-layouts  18 us (13%)
    ppermute x9, waiting for transfers between devices, exchanged(): lax.ppermute(part, 'ent', [(i, i ^ stride) for i in range(ends)])  35.5 us
    pallas_call x9, Pallas kernels, call(): pl.pallas_call(kernel, in_specs=[SMEM] * smem + [VMEM] * (len(operands) -...  31.7 us
    ppermute x9, starting transfers between devices, exchanged(): lax.ppermute(part, 'ent', [(i, i ^ stride) for i in range(ends)])  20.2 us
    unnamed x42, local copies, waits for them, and re-layouts  17.3 us
    pallas_call x1, Pallas kernels, body(): pl.pallas_call(functools.partial(prep_kernel, plan, blocks, splits, layer...  14.1 us
    ppermute x3, starting transfers between devices, shifts(): left = lax.ppermute(cells, 'ent', [(i, i + 1) for i in range(ends - 1)])  8.45 us
    ppermute x3, starting transfers between devices, shifts(): right = lax.ppermute(cells, 'ent', [(i + 1, i) for i in range(ends - 1)])  3.88 us
    all_to_all x1, starting transfers between devices, body(): lax.all_to_all(states, 'qry', split_axis=1, concat_axis=0, tiled=True)  3.25 us
  transfers between devices with their start and end apart: 16, of which 7 were waited for; matrix products, arithmetic and copies ran while one was open for 0% of the time, Pallas kernels for 28%

profile of v2, /device:TPU:0, one launch (start us, length us, event | category | flops | bytes accessed | tf_op | source)
XLA Modules:
  0.0 138.7 jit_solution(9050424788085023410)
XLA Ops:
  0.6 4.9 %collective-permute-start = (bf16[64,1024]{1,0:T(8,128)(2,1)}, bf16[64,1024]{1,0:T(8,128)(2,1)S(1)}, u32[]{:S(2)}, u32[]{:S(2)}) collective-permute-start(bf16[64,1024]{1,0:T(8,128)(2,1)} %refs_0_.1), channel_id=1, source_target_pairs={{0,4},{4,8},{8,12},{12,16},{16,20},{20,24},{24,28},{1,5},{5,9},{9,... | collective-permute-start | bytes 393224 | tf_op jit(solution)/shard_map/ppermute | solution.py:452
  6.8 2.5 %copy-done = s32[80,128,128]{2,1,0:T(8,128)S(1)} copy-done((s32[80,128,128]{2,1,0:T(8,128)S(1)}, s32[80,128,128]{2,1,0:T(8,128)}, u32[]{:S(2)}) %copy-start) | copy-done | bytes 5242904
  24.2 14.1 %prep.1 = (bf16[128,128,128]{2,1,0:T(8,128)(2,1)S(1)}, f32[3,136,256]{2,1,0:T(8,128)S(1)}, f32[16,256]{1,0:T(8,128)S(1)}, s32[8,256]{1,0:T(8,128)S(1)}, bf16[5,2...) custom-call(s32[2,80]{1,0:T(2,128)S(1)} %bitcast.17, s32[2,24]{1,0:T(2,128)S(1)} %bitcast.18, s32[2,24]{1,0:T(2,128)S(1)} %bitcast.19, ...), custom_call_target="tpu_custom_call" | custom-call | bytes 12582912 | tf_op jit(solution)/shard_map/prep/pallas_call | solution.py:426
  38.3 2.3 %own.3 = (bf16[1024,256]{1,0:T(8,128)(2,1)S(1)}, f32[1024,256]{1,0:T(8,128)S(1)}, f32[128,256]{1,0:T(8,128)S(1)}) custom-call(s32[763]{0:T(1024)S(1)} %get-tuple-element.28.order, bf16[128,128,128]{2,1,0:T(8,128)(2,1)S(1)} %get-tuple-element.29.turned, f32[3,136,256]{2,1,0:T(8,128)S(1)} %get-tuple-element.30.rel_rows, bf16[64,1024]{1,0:T(8,128)(2,1)S(1)} %copy-done.4, ...), custom_call_target="tpu_custom_call" | custom-call | flops 536870912 | bytes 4194304 | tf_op jit(solution)/shard_map/own/pallas_call | solution.py:464
  40.7 2.7 %collective-permute-start.2 = (f32[128,256]{1,0:T(8,128)S(1)}, f32[128,256]{1,0:T(8,128)S(1)}, u32[]{:S(2)}, u32[]{:S(2)}) collective-permute-start(f32[128,256]{1,0:T(8,128)S(1)} %get-tuple-element.39), channel_id=1, source_target_pairs={{0,4},{4,0},{8,12},{12,8},{16,20},{20,16},{24,28},{28,24},{1,5},{5... | collective-permute-start | bytes 393224 | tf_op jit(solution)/shard_map/ppermute | solution.py:458
  43.4 6.7 %close.3.refs_0_.own = bf16[1024,256]{1,0:T(8,128)(2,1)S(1)} custom-call(s32[763]{0:T(1024)S(1)} %get-tuple-element.28.order, bf16[128,128,128]{2,1,0:T(8,128)(2,1)S(1)} %get-tuple-element.29.turned, f32[3,136,256]{2,1,0:T(8,128)S(1)} %get-tuple-element.30.rel_rows, f32[16,256]{1,0:T(8,128)S(1)} %get-tuple-element.31.refs_1_.lane_rows, ...), custom_call_target="tpu_custom_call" | custom-call | flops 536870912 | bytes 4194304 | tf_op jit(solution)/shard_map/close/pallas_call | solution.py:464
  50.1 1.8 %collective-permute-start.5 = (bf16[1024,256]{1,0:T(8,128)(2,1)S(1)}, bf16[1024,256]{1,0:T(8,128)(2,1)S(1)}, u32[]{:S(2)}, u32[]{:S(2)}) collective-permute-start(bf16[1024,256]{1,0:T(8,128)(2,1)S(1)} %close.3.refs_0_.own), channel_id=1, source_target_pairs={{0,4},{4,8},{8,12},{12,16},{16,20},{20,24},{24,28},{1,5},{5,9},{9,... | collective-permute-start | bytes 1572872 | tf_op jit(solution)/shard_map/ppermute | solution.py:452
  53.3 5.3 %collective-permute-start.3 = (f32[128,256]{1,0:T(8,128)S(1)}, f32[128,256]{1,0:T(8,128)S(1)}, u32[]{:S(2)}, u32[]{:S(2)}) collective-permute-start(f32[128,256]{1,0:T(8,128)S(1)} %add.27), channel_id=1, source_target_pairs={{0,8},{4,12},{8,0},{12,4},{16,24},{20,28},{24,16},{28,20},{1,9},{5... | collective-permute-start | bytes 393224 | tf_op jit(solution)/shard_map/ppermute | solution.py:458
  58.5 13.3 %collective-permute-done.3 = f32[128,256]{1,0:T(8,128)S(1)} collective-permute-done((f32[128,256]{1,0:T(8,128)S(1)}, f32[128,256]{1,0:T(8,128)S(1)}, u32[]{:S(2)}, u32[]{:S(2)}) %collective-permute-start.3) | collective-permute-done | bytes 131104 | tf_op jit(solution)/shard_map/ppermute | solution.py:458
  71.9 4.9 %collective-permute-start.4 = (f32[128,256]{1,0:T(8,128)S(1)}, f32[128,256]{1,0:T(8,128)S(1)}, u32[]{:S(2)}, u32[]{:S(2)}) collective-permute-start(f32[128,256]{1,0:T(8,128)S(1)} %add.28), channel_id=1, source_target_pairs={{0,16},{4,20},{8,24},{12,28},{16,0},{20,4},{24,8},{28,12},{1,17},{... | collective-permute-start | bytes 393224 | tf_op jit(solution)/shard_map/ppermute | solution.py:458
  76.8 1.8 %own.4 = (f32[1024,256]{1,0:T(8,128)S(1)}, f32[128,256]{1,0:T(8,128)S(1)}) custom-call(s32[763]{0:T(1024)S(1)} %get-tuple-element.28.order, bf16[128,128,128]{2,1,0:T(8,128)(2,1)S(1)} %get-tuple-element.29.turned, f32[3,136,256]{2,1,0:T(8,128)S(1)} %get-tuple-element.30.rel_rows, bf16[1024,256]{1,0:T(8,128)(2,1)S(1)} %close.3.refs_0_.own), custom_call_target="tpu_custom_call" | custom-call | flops 536870912 | bytes 4194304 | tf_op jit(solution)/shard_map/own/pallas_call | solution.py:464
  80.1 1.8 %hout.2 = (f32[1024,256]{1,0:T(8,128)S(1)}, bf16[128,256]{1,0:T(8,128)(2,1)S(1)}) custom-call(s32[763]{0:T(1024)S(1)} %get-tuple-element.28.order, bf16[128,128,128]{2,1,0:T(8,128)(2,1)S(1)} %get-tuple-element.29.turned, f32[3,136,256]{2,1,0:T(8,128)S(1)} %get-tuple-element.30.rel_rows, f32[16,256]{1,0:T(8,128)S(1)} %get-tuple-element.31.refs_1_.lane_rows, ...), custom_call_target="tpu_custom_call" | custom-call | flops 268435456 | bytes 2097152 | tf_op jit(solution)/shard_map/hout/pallas_call | solution.py:464
  82.0 5.0 %collective-permute-done.7 = f32[128,256]{1,0:T(8,128)S(1)} collective-permute-done((f32[128,256]{1,0:T(8,128)S(1)}, f32[128,256]{1,0:T(8,128)S(1)}, u32[]{:S(2)}, u32[]{:S(2)}) %collective-permute-start.7) | collective-permute-done | bytes 131104 | tf_op jit(solution)/shard_map/ppermute | solution.py:458
  87.0 6.5 %close.4.refs_0_.own = bf16[1024,256]{1,0:T(8,128)(2,1)S(1)} custom-call(s32[763]{0:T(1024)S(1)} %get-tuple-element.28.order, bf16[128,128,128]{2,1,0:T(8,128)(2,1)S(1)} %get-tuple-element.29.turned, f32[3,136,256]{2,1,0:T(8,128)S(1)} %get-tuple-element.30.rel_rows, f32[16,256]{1,0:T(8,128)S(1)} %get-tuple-element.31.refs_1_.lane_rows, ...), custom_call_target="tpu_custom_call" | custom-call | flops 536870912 | bytes 4194304 | tf_op jit(solution)/shard_map/close/pallas_call | solution.py:464
  93.5 1.8 %collective-permute-start.10 = (bf16[1024,256]{1,0:T(8,128)(2,1)S(1)}, bf16[1024,256]{1,0:T(8,128)(2,1)S(1)}, u32[]{:S(2)}, u32[]{:S(2)}) collective-permute-start(bf16[1024,256]{1,0:T(8,128)(2,1)S(1)} %close.4.refs_0_.own), channel_id=1, source_target_pairs={{0,4},{4,8},{8,12},{12,16},{16,20},{20,24},{24,28},{1,5},{5,9},{9,... | collective-permute-start | bytes 1572872 | tf_op jit(solution)/shard_map/ppermute | solution.py:452
  98.4 2.8 %collective-permute-start.12 = (f32[128,256]{1,0:T(8,128)S(1)}, f32[128,256]{1,0:T(8,128)S(1)}, u32[]{:S(2)}, u32[]{:S(2)}) collective-permute-start(f32[128,256]{1,0:T(8,128)S(1)} %get-tuple-element.52), channel_id=1, source_target_pairs={{0,8},{4,12},{8,0},{12,4},{16,24},{20,28},{24,16},{28,20},{1,9},{5... | collective-permute-start | bytes 393224 | tf_op jit(solution)/shard_map/ppermute | solution.py:458
  101.2 10.9 %collective-permute-done.12 = f32[128,256]{1,0:T(8,128)S(1)} collective-permute-done((f32[128,256]{1,0:T(8,128)S(1)}, f32[128,256]{1,0:T(8,128)S(1)}, u32[]{:S(2)}, u32[]{:S(2)}) %collective-permute-start.12) | collective-permute-done | bytes 131104 | tf_op jit(solution)/shard_map/ppermute | solution.py:458
  112.1 3.0 %collective-permute-start.13 = (f32[128,256]{1,0:T(8,128)S(1)}, f32[128,256]{1,0:T(8,128)S(1)}, u32[]{:S(2)}, u32[]{:S(2)}) collective-permute-start(f32[128,256]{1,0:T(8,128)S(1)} %add.33), channel_id=1, source_target_pairs={{0,16},{4,20},{8,24},{12,28},{16,0},{20,4},{24,8},{28,12},{1,17},{... | collective-permute-start | bytes 393224 | tf_op jit(solution)/shard_map/ppermute | solution.py:458
  116.5 2.2 %collective-permute-done.13 = f32[128,256]{1,0:T(8,128)S(1)} collective-permute-done((f32[128,256]{1,0:T(8,128)S(1)}, f32[128,256]{1,0:T(8,128)S(1)}, u32[]{:S(2)}, u32[]{:S(2)}) %collective-permute-start.13) | collective-permute-done | bytes 131104 | tf_op jit(solution)/shard_map/ppermute | solution.py:458
  118.8 2.7 %collective-permute-done.9 = f32[128,256]{1,0:T(8,128)S(1)} collective-permute-done((f32[128,256]{1,0:T(8,128)S(1)}, f32[128,256]{1,0:T(8,128)S(1)}, u32[]{:S(2)}, u32[]{:S(2)}) %collective-permute-start.9) | collective-permute-done | bytes 131104 | tf_op jit(solution)/shard_map/ppermute | solution.py:458
  121.5 1.8 %hout.3 = (f32[1024,256]{1,0:T(8,128)S(1)}, bf16[128,256]{1,0:T(8,128)(2,1)S(1)}) custom-call(s32[763]{0:T(1024)S(1)} %get-tuple-element.28.order, bf16[128,128,128]{2,1,0:T(8,128)(2,1)S(1)} %get-tuple-element.29.turned, f32[3,136,256]{2,1,0:T(8,128)S(1)} %get-tuple-element.30.rel_rows, f32[16,256]{1,0:T(8,128)S(1)} %get-tuple-element.31.refs_1_.lane_rows, ...), custom_call_target="tpu_custom_call" | custom-call | flops 268435456 | bytes 2097152 | tf_op jit(solution)/shard_map/hout/pallas_call | solution.py:464
  123.3 7.6 %close.5 = f32[4,1024]{1,0:T(4,128)} custom-call(s32[763]{0:T(1024)S(1)} %get-tuple-element.28.order, bf16[128,128,128]{2,1,0:T(8,128)(2,1)S(1)} %get-tuple-element.29.turned, f32[3,136,256]{2,1,0:T(8,128)S(1)} %get-tuple-element.30.rel_rows, f32[16,256]{1,0:T(8,128)S(1)} %get-tuple-element.31.refs_1_.lane_rows, ...), custom_call_target="tpu_custom_call" | custom-call | flops 536870912 | bytes 4194304 | tf_op jit(solution)/shard_map/close/pallas_call | solution.py:464
  131.0 3.3 %all-to-all-start = ((f32[4,4,256]{2,0,1:T(4,128)}), f32[4,4,256]{2,0,1:T(4,128)S(1)}, u32[]{:S(2)}, u32[]{:S(2)}) async-start(f32[4,4,256]{2,0,1:T(4,128)} %bitcast.12), calls=%async_computation | async-start | bytes 32768 | tf_op jit(solution)/shard_map/all_to_all | solution.py:532
  135.6 2.5 %all-to-all-done = f32[4,4,256]{2,0,1:T(4,128)S(1)} async-done(((f32[4,4,256]{2,0,1:T(4,128)}), f32[4,4,256]{2,0,1:T(4,128)S(1)}, u32[]{:S(2)}, u32[]{:S(2)}) %all-to-all-start) | async-done | bytes 16416 | tf_op jit(solution)/shard_map/all_to_all | solution.py:532
  (70 shorter events, 25.7 us)
Async XLA Ops:
  0.6 40.0 %collective-permute-start = (bf16[64,1024]{1,0:T(8,128)(2,1)}, bf16[64,1024]{1,0:T(8,128)(2,1)S(1)}, u32[]{:S(2)}, u32[]{:S(2)}) collective-permute-start(bf16[64,1024]{1,0:T(8,128)(2,1)} %refs_0_.1), channel_id=1, source_target_pairs={{0,4},{4,8},{8,12},{12,16},{16,20},{20,24},{24,28},{1,5},{5,9},{9,... | collective-permute-start | bytes 393224 | tf_op jit(solution)/shard_map/ppermute | solution.py:452
  5.5 35.2 %collective-permute-start.1 = (bf16[64,1024]{1,0:T(8,128)(2,1)}, bf16[64,1024]{1,0:T(8,128)(2,1)S(1)}, u32[]{:S(2)}, u32[]{:S(2)}) collective-permute-start(bf16[64,1024]{1,0:T(8,128)(2,1)} %refs_0_.1), channel_id=1, source_target_pairs={{4,0},{8,4},{12,8},{16,12},{20,16},{24,20},{28,24},{5,1},{9,5},{13... | collective-permute-start | bytes 393224 | tf_op jit(solution)/shard_map/ppermute | solution.py:453
  6.8 2.5 %copy-start = (s32[80,128,128]{2,1,0:T(8,128)S(1)}, s32[80,128,128]{2,1,0:T(8,128)}, u32[]{:S(2)}) copy-start(s32[80,128,128]{2,1,0:T(8,128)} %reg_mask.1) | copy-start | bytes 15728644
  9.3 1.4 %copy-start.1 = (s32[24,128,128]{2,1,0:T(8,128)S(1)}, s32[24,128,128]{2,1,0:T(8,128)}, u32[]{:S(2)}) copy-start(s32[24,128,128]{2,1,0:T(8,128)} %hin_mask.1) | copy-start | bytes 4718596
  10.7 1.4 %copy-start.2 = (s32[24,128,128]{2,1,0:T(8,128)S(1)}, s32[24,128,128]{2,1,0:T(8,128)}, u32[]{:S(2)}) copy-start(s32[24,128,128]{2,1,0:T(8,128)} %hout_mask.1) | copy-start | bytes 4718596
  12.1 1.0 copy-start.3
  13.1 0.9 copy-start.5
  14.0 0.8 copy-start.6
  14.8 0.7 copy-start.7
  24.2 14.1 %copy-start.4 = (bf16[64,1024]{1,0:T(8,128)(2,1)S(1)}, bf16[64,1024]{1,0:T(8,128)(2,1)}, u32[]{:S(2)}) copy-start(bf16[64,1024]{1,0:T(8,128)(2,1)} %refs_0_.1) | copy-start | bytes 393220
  40.7 9.4 %collective-permute-start.2 = (f32[128,256]{1,0:T(8,128)S(1)}, f32[128,256]{1,0:T(8,128)S(1)}, u32[]{:S(2)}, u32[]{:S(2)}) collective-permute-start(f32[128,256]{1,0:T(8,128)S(1)} %get-tuple-element.39), channel_id=1, source_target_pairs={{0,4},{4,0},{8,12},{12,8},{16,20},{20,16},{24,28},{28,24},{1,5},{5... | collective-permute-start | bytes 393224 | tf_op jit(solution)/shard_map/ppermute | solution.py:458
  50.1 36.9 %collective-permute-start.5 = (bf16[1024,256]{1,0:T(8,128)(2,1)S(1)}, bf16[1024,256]{1,0:T(8,128)(2,1)S(1)}, u32[]{:S(2)}, u32[]{:S(2)}) collective-permute-start(bf16[1024,256]{1,0:T(8,128)(2,1)S(1)} %close.3.refs_0_.own), channel_id=1, source_target_pairs={{0,4},{4,8},{8,12},{12,16},{16,20},{20,24},{24,28},{1,5},{5,9},{9,... | collective-permute-start | bytes 1572872 | tf_op jit(solution)/shard_map/ppermute | solution.py:452
  52.0 35.1 %collective-permute-start.6 = (bf16[1024,256]{1,0:T(8,128)(2,1)S(1)}, bf16[1024,256]{1,0:T(8,128)(2,1)S(1)}, u32[]{:S(2)}, u32[]{:S(2)}) collective-permute-start(bf16[1024,256]{1,0:T(8,128)(2,1)S(1)} %close.3.refs_0_.own), channel_id=1, source_target_pairs={{4,0},{8,4},{12,8},{16,12},{20,16},{24,20},{28,24},{5,1},{9,5},{13... | collective-permute-start | bytes 1572872 | tf_op jit(solution)/shard_map/ppermute | solution.py:453
  53.3 18.6 %collective-permute-start.3 = (f32[128,256]{1,0:T(8,128)S(1)}, f32[128,256]{1,0:T(8,128)S(1)}, u32[]{:S(2)}, u32[]{:S(2)}) collective-permute-start(f32[128,256]{1,0:T(8,128)S(1)} %add.27), channel_id=1, source_target_pairs={{0,8},{4,12},{8,0},{12,4},{16,24},{20,28},{24,16},{28,20},{1,9},{5... | collective-permute-start | bytes 393224 | tf_op jit(solution)/shard_map/ppermute | solution.py:458
  71.9 8.2 %collective-permute-start.4 = (f32[128,256]{1,0:T(8,128)S(1)}, f32[128,256]{1,0:T(8,128)S(1)}, u32[]{:S(2)}, u32[]{:S(2)}) collective-permute-start(f32[128,256]{1,0:T(8,128)S(1)} %add.28), channel_id=1, source_target_pairs={{0,16},{4,20},{8,24},{12,28},{16,0},{20,4},{24,8},{28,12},{1,17},{... | collective-permute-start | bytes 393224 | tf_op jit(solution)/shard_map/ppermute | solution.py:458
  82.0 5.0 %collective-permute-start.7 = (f32[128,256]{1,0:T(8,128)S(1)}, f32[128,256]{1,0:T(8,128)S(1)}, u32[]{:S(2)}, u32[]{:S(2)}) collective-permute-start(f32[128,256]{1,0:T(8,128)S(1)} %get-tuple-element.46), channel_id=1, source_target_pairs={{0,4},{4,0},{8,12},{12,8},{16,20},{20,16},{24,28},{28,24},{1,5},{5... | collective-permute-start | bytes 393224 | tf_op jit(solution)/shard_map/ppermute | solution.py:458
  93.5 29.8 %collective-permute-start.10 = (bf16[1024,256]{1,0:T(8,128)(2,1)S(1)}, bf16[1024,256]{1,0:T(8,128)(2,1)S(1)}, u32[]{:S(2)}, u32[]{:S(2)}) collective-permute-start(bf16[1024,256]{1,0:T(8,128)(2,1)S(1)} %close.4.refs_0_.own), channel_id=1, source_target_pairs={{0,4},{4,8},{8,12},{12,16},{16,20},{20,24},{24,28},{1,5},{5,9},{9,... | collective-permute-start | bytes 1572872 | tf_op jit(solution)/shard_map/ppermute | solution.py:452
  95.3 28.0 %collective-permute-start.11 = (bf16[1024,256]{1,0:T(8,128)(2,1)S(1)}, bf16[1024,256]{1,0:T(8,128)(2,1)S(1)}, u32[]{:S(2)}, u32[]{:S(2)}) collective-permute-start(bf16[1024,256]{1,0:T(8,128)(2,1)S(1)} %close.4.refs_0_.own), channel_id=1, source_target_pairs={{4,0},{8,4},{12,8},{16,12},{20,16},{24,20},{28,24},{5,1},{9,5},{13... | collective-permute-start | bytes 1572872 | tf_op jit(solution)/shard_map/ppermute | solution.py:453
  98.4 13.7 %collective-permute-start.12 = (f32[128,256]{1,0:T(8,128)S(1)}, f32[128,256]{1,0:T(8,128)S(1)}, u32[]{:S(2)}, u32[]{:S(2)}) collective-permute-start(f32[128,256]{1,0:T(8,128)S(1)} %get-tuple-element.52), channel_id=1, source_target_pairs={{0,8},{4,12},{8,0},{12,4},{16,24},{20,28},{24,16},{28,20},{1,9},{5... | collective-permute-start | bytes 393224 | tf_op jit(solution)/shard_map/ppermute | solution.py:458
  101.1 13.9 %collective-permute-start.8 = (f32[128,256]{1,0:T(8,128)S(1)}, f32[128,256]{1,0:T(8,128)S(1)}, u32[]{:S(2)}, u32[]{:S(2)}) collective-permute-start(f32[128,256]{1,0:T(8,128)S(1)} %add.30), channel_id=1, source_target_pairs={{0,8},{4,12},{8,0},{12,4},{16,24},{20,28},{24,16},{28,20},{1,9},{5... | collective-permute-start | bytes 393224 | tf_op jit(solution)/shard_map/ppermute | solution.py:458
  112.1 6.5 %collective-permute-start.13 = (f32[128,256]{1,0:T(8,128)S(1)}, f32[128,256]{1,0:T(8,128)S(1)}, u32[]{:S(2)}, u32[]{:S(2)}) collective-permute-start(f32[128,256]{1,0:T(8,128)S(1)} %add.33), channel_id=1, source_target_pairs={{0,16},{4,20},{8,24},{12,28},{16,0},{20,4},{24,8},{28,12},{1,17},{... | collective-permute-start | bytes 393224 | tf_op jit(solution)/shard_map/ppermute | solution.py:458
  115.1 6.3 %collective-permute-start.9 = (f32[128,256]{1,0:T(8,128)S(1)}, f32[128,256]{1,0:T(8,128)S(1)}, u32[]{:S(2)}, u32[]{:S(2)}) collective-permute-start(f32[128,256]{1,0:T(8,128)S(1)} %add.31), channel_id=1, source_target_pairs={{0,16},{4,20},{8,24},{12,28},{16,0},{20,4},{24,8},{28,12},{1,17},{... | collective-permute-start | bytes 393224 | tf_op jit(solution)/shard_map/ppermute | solution.py:458
  118.7 15.6 %collective-permute-start.14 = (f32[128,256]{1,0:T(8,128)S(1)}, f32[128,256]{1,0:T(8,128)S(1)}, u32[]{:S(2)}, u32[]{:S(2)}) collective-permute-start(f32[128,256]{1,0:T(8,128)S(1)} %add.34), channel_id=1, source_target_pairs={{0,4},{4,0},{8,12},{12,8},{16,20},{20,16},{24,28},{28,24},{1,5},{5... | collective-permute-start | bytes 393224 | tf_op jit(solution)/shard_map/ppermute | solution.py:458
  131.0 7.1 %all-to-all-start = ((f32[4,4,256]{2,0,1:T(4,128)}), f32[4,4,256]{2,0,1:T(4,128)S(1)}, u32[]{:S(2)}, u32[]{:S(2)}) async-start(f32[4,4,256]{2,0,1:T(4,128)} %bitcast.12), calls=%async_computation | async-start | bytes 32768 | tf_op jit(solution)/shard_map/all_to_all | solution.py:532
  (13 other events, 8.7 us)

commit v3 on v2

v3 whole, which is shorter than its diff:
```python
import functools
import math

import jax
import jax.numpy as jnp
from jax import lax
from jax.experimental import pallas as pl
from jax.experimental.pallas import tpu as pltpu
from jax.sharding import PartitionSpec as P


HUB_DEV = 16
F32 = jnp.float32
BF16 = jnp.bfloat16
SMEM = pl.BlockSpec(memory_space=pltpu.SMEM)
VMEM = pl.BlockSpec(memory_space=pltpu.VMEM)
LEFT, OWN, RIGHT, HOUT, HIN = range(5)


class Plan:
    def __init__(self, counts, blocks, hub_blocks):
        reg, hin, hout = counts
        self.tiles = reg + hin + hout
        self.keys = [blocks, blocks, blocks, blocks, hub_blocks]
        mean = [reg / (3 * blocks)] * 3 + [hout / blocks, hin / hub_blocks]
        most = [reg] * 3 + [hout, hin]
        self.slots = [
            min(m + m % 2, 2 * math.ceil((a + 1.2 * math.sqrt(a)) / 2)) for a, m in zip(mean, most)
        ]
        self.first_key = [sum(self.keys[:s]) for s in range(5)]
        place = 16
        self.main = []
        for side in range(5):
            self.main.append(place)
            place += self.keys[side] * self.slots[side]
        self.more = []
        for side in range(5):
            self.more.append(place)
            place += most[side]
        self.size = place


def spreader(width, lanes, transposed=False):
    shape = (lanes, width) if transposed else (width, lanes)
    row = lax.broadcasted_iota(jnp.int32, shape, 0)
    column = lax.broadcasted_iota(jnp.int32, shape, 1)
    hit = lax.rem(row, width) == column if transposed else lax.rem(column, width) == row
    return hit.astype(F32).astype(BF16)


def contract_last(a, b):
    return lax.dot_general(a, b, (((1,), (1,)), ((), ())), preferred_element_type=F32)


def prep_kernel(plan, blocks, layers, *refs):
    count = 20
    sources, refs = refs[:count], refs[count:]
    turned, rel_rows, lane_rows, lane_heads, weights, order = refs[:6]
    landed = refs[6 : 6 + count]
    stack, q_rows, count_of, used, sems = refs[6 + count :]
    copies = [pltpu.make_async_copy(a, b, sems.at[i]) for i, (a, b) in enumerate(zip(sources, landed))]
    for copy in copies:
        copy.start()
    (
        reg_blocks, hin_blocks, hout_blocks, query_head, query_rel, reg_rel, hin_rel, hout_rel,
        query_table, rel_table, read_weight, read_bias, read_out, layer_weight, layer_bias, norm_gain,
        norm_shift, *masks,
    ) = landed
    width, relations = query_table.shape
    lanes = lane_rows.shape[1]
    q_local = lanes // width
    block = turned.shape[1]
    queries = query_rel.shape[1]
    first_block = lax.axis_index("ent") * blocks
    query_first = lax.axis_index("qry") * q_local
    empty = plan.tiles

    for key in range(sum(plan.keys)):
        count_of[key] = 0
    for side in range(5):
        used[side] = 0

    def clear(i, _):
        order[i] = empty
        return 0

    lax.fori_loop(plan.main[0], plan.more[0], clear, 0, unroll=8)
    spread = spreader(width, lanes)
    spread_back = spreader(width, lanes, True)
    same = lax.div(lax.broadcasted_iota(jnp.int32, (lanes, lanes), 0), width) == lax.div(
        lax.broadcasted_iota(jnp.int32, (lanes, lanes), 1), width
    )
    weights[2 * layers + 1] = jnp.where(same, 1.0 / width, 0.0).astype(BF16)
    for copy in copies[:17]:
        copy.wait()

    def picked(table, ids):
        row = lax.broadcasted_iota(jnp.int32, (relations, ids.shape[1]), 0)
        hit = (row == ids[...]).astype(F32).astype(BF16)
        return jnp.transpose(jnp.dot(table, hit, preferred_element_type=F32)).astype(BF16)

    base = 0
    for ids in (reg_rel, hin_rel, hout_rel):
        rows = picked(rel_table[...].reshape(layers * width, relations), ids)
        for layer in range(layers):
            rel_rows[layer, base : base + ids.shape[1], :] = jnp.dot(
                rows[:, layer * width : (layer + 1) * width], spread, preferred_element_type=F32
            )
        base += ids.shape[1]
    for layer in range(layers):
        rel_rows[layer, base:, :] = jnp.zeros((rel_rows.shape[1] - base, lanes), F32)

    def centred(rows):
        return rows - jnp.mean(rows, axis=1, keepdims=True)

    q_rows[...] = picked(query_table[...], query_rel).astype(F32)
    own = q_rows[...].astype(BF16)
    stack[...] = jnp.zeros_like(stack)
    stack[0:queries, :] = contract_last(own, read_weight[:, width:]) + read_bias[...]
    for at, rows in ((1, layer_bias), (1 + layers, norm_gain), (1 + 2 * layers, norm_shift)):
        values = centred(rows[...]) if at == 1 else rows[...]
        stack[queries + at : queries + at + layers, :] = values
    stack[queries : queries + 1, :] = read_out[...]
    wide = jnp.dot(stack[...], spread.astype(F32), precision=lax.Precision.HIGHEST)
    q_of_lane = lax.div(lax.broadcasted_iota(jnp.int32, (1, lanes), 1), width)
    wide_q = jnp.dot(own, spread, preferred_element_type=F32)
    mine = lax.broadcasted_iota(jnp.int32, wide_q.shape, 0) - query_first == q_of_lane
    lane_rows[...] = jnp.zeros_like(lane_rows)
    lane_rows[0:1, :] = jnp.sum(jnp.where(mine, wide_q, 0.0), axis=0, keepdims=True)
    lane_rows[1:2, :] = jnp.sum(jnp.where(mine, wide[:queries], 0.0), axis=0, keepdims=True)
    lane_rows[2 : 3 + 3 * layers, :] = wide[queries : queries + 1 + 3 * layers]
    lane_head = jnp.zeros((1, lanes), jnp.int32)
    for q in range(q_local):
        lane_head = jnp.where(q_of_lane == q, query_head[query_first + q], lane_head)
    lane_heads[...] = jnp.broadcast_to(lane_head, lane_heads.shape)

    def put_weight(at, tall):
        full = jnp.dot(tall.astype(BF16), spread, preferred_element_type=F32)
        weights[at] = jnp.where(same, full, 0.0).astype(BF16)

    for layer in range(layers):
        level = centred(layer_weight[layer].astype(F32))
        high = level.astype(BF16)
        low = (level - high.astype(F32)).astype(BF16)
        for part, value in enumerate((high, low)):
            put_weight(2 * layer + part, jnp.dot(spread_back, value, preferred_element_type=F32))
    put_weight(2 * layers, contract_last(spread_back, read_weight[:, :width]))

    eye = lax.broadcasted_iota(jnp.int32, (block, block), 0) == lax.broadcasted_iota(
        jnp.int32, (block, block), 1
    )
    eye = eye.astype(F32).astype(BF16)

    def note(tile, side, local, source, slots, main, more, key):
        seen = count_of[key]
        count_of[key] = seen + 1
        rest = used[side]
        fits = seen < slots
        used[side] = rest + jnp.where(fits, 0, 1)
        order[jnp.where(fits, main + local * slots + seen, more + rest)] = (
            tile + source * 4096 + local * (1 << 21)
        )

    def note_reg(t, tile):
        place = reg_blocks[1, t] - first_block + blocks
        side = lax.div(place, blocks)
        local = reg_blocks[0, t] - first_block
        note(
            tile, side, local, place - side * blocks, plan.slots[0],
            plan.main[0] + side * (plan.main[1] - plan.main[0]),
            plan.more[0] + side * (plan.more[1] - plan.more[0]), side * blocks + local,
        )

    def note_hin(t, tile):
        local = hin_blocks[0, t]
        note(
            tile, HIN, local, hin_blocks[1, t] - first_block, plan.slots[HIN], plan.main[HIN],
            plan.more[HIN], plan.first_key[HIN] + local,
        )

    def note_hout(t, tile):
        local = hout_blocks[0, t] - first_block
        note(
            tile, HOUT, local, hout_blocks[1, t], plan.slots[HOUT], plan.main[HOUT],
            plan.more[HOUT], plan.first_key[HOUT] + local,
        )

    base = 0
    for copy, mask, put in zip(copies[17:], masks, (note_reg, note_hin, note_hout)):
        copy.wait()
        count = mask.shape[0]
        group = math.gcd(count, 8)

        def turn(g, _, mask=mask, put=put, base=base, group=group):
            for u in range(group):
                t = g * group + u
                turned[base + t] = contract_last(eye, mask[t].astype(F32).astype(BF16)).astype(BF16)
                put(t, base + t)
            return 0

        lax.fori_loop(0, count // group, turn, 0)
        base += count
    for side in range(5):
        order[side] = used[side]


def slot_product(plan, layer, order, turned, rel_rows, places):
    block = turned.shape[1]
    lanes = rel_rows.shape[2]
    masks, values = [], []
    for place, source in places:
        word = order[place]
        tile = word & 4095
        start = pl.multiple_of(((word >> 12) & 511) * block, block)
        row = jnp.broadcast_to(rel_rows[layer, pl.ds(tile, 1), :], (16, lanes)).astype(BF16)
        value = source[pl.ds(start, block), :].reshape(block // 16, 16, lanes)
        values.append((value * row[None]).reshape(block, lanes))
        masks.append(turned[jnp.where(tile == plan.tiles, 0, tile)])
    return jnp.dot(
        jnp.concatenate(masks, axis=1), jnp.concatenate(values, axis=0), preferred_element_type=F32
    )


def key_product(plan, layer, side_sources, key, order, turned, rel_rows):
    total = None
    for side, source in side_sources:
        slots = plan.slots[side]
        for start in range(0, slots, 6):
            places = [
                (plan.main[side] + key * slots + u, source) for u in range(start, min(start + 6, slots))
            ]
            product = slot_product(plan, layer, order, turned, rel_rows, places)
            total = product if total is None else total + product
    return total


def add_rest(plan, layer, side, source, order, turned, rel_rows, total):
    block = turned.shape[1]

    def one(i, _):
        at = plan.more[side] + i
        place = pl.ds(pl.multiple_of((order[at] >> 21) * block, block), block)
        total[place, :] += slot_product(plan, layer, order, turned, rel_rows, [(at, source)])
        return 0

    lax.fori_loop(0, order[side], one, 0)


def normed_step(inputs, layer, layers, weights, lane_rows):
    bias, gain, shift = (lane_rows[3 + layer + i * layers : 4 + layer + i * layers, :] for i in range(3))
    centered = (
        jnp.dot(inputs, weights[2 * layer], preferred_element_type=F32)
        + jnp.dot(inputs, weights[2 * layer + 1], preferred_element_type=F32)
        + bias
    )
    squares = (centered * centered).astype(BF16)
    variance = jnp.dot(squares, weights[2 * layers + 1], preferred_element_type=F32)
    return jnp.maximum(centered * lax.rsqrt(variance + 1e-05) * gain + shift, 0.0)


def hit_lanes(rows, first, heads, values):
    place = first + lax.broadcasted_iota(jnp.int32, (rows, heads.shape[1]), 0)
    return jnp.where(place == heads, values, 0.0)


def first_states(feat, first, block, lane_rows, lane_heads, out):
    width, count = feat.shape
    columns = jnp.transpose(feat[...].astype(F32)).astype(BF16)
    spread = spreader(width, out.shape[1])
    for start in range(0, count, block):
        wide = jnp.dot(columns[start : start + block, :], spread, preferred_element_type=F32)
        hits = hit_lanes(block, first + start, lane_heads[0:1, :], lane_rows[0:1, :])
        out[start : start + block, :] = (wide + hits).astype(BF16)


def own_kernel(plan, layer, order, turned, rel_rows, *refs):
    block = turned.shape[1]
    if layer == 0:
        feat, lane_rows, lane_heads, states, total, hub_part = refs
        first = lax.axis_index("ent") * feat.shape[1]
        first_states(feat, first, block, lane_rows, lane_heads, states)
    else:
        states, total, hub_part = refs
    for side, out in ((HIN, hub_part), (OWN, total)):
        for key in range(plan.keys[side]):
            out[key * block : (key + 1) * block, :] = key_product(
                plan, layer, ((side, states),), key, order, turned, rel_rows
            )
        add_rest(plan, layer, side, states, order, turned, rel_rows, out)


def side_kernel(block, left_feat, right_feat, lane_rows, lane_heads, left, right):
    count = left_feat.shape[1]
    first = lax.axis_index("ent") * count
    first_states(left_feat, first - count, block, lane_rows, lane_heads, left)
    first_states(right_feat, first + count, block, lane_rows, lane_heads, right)


def update_hubs(hub_sum, hub_old, layer, layers, weights, lane_rows):
    inputs = (hub_sum * lane_rows[0:1, :]).astype(BF16)
    grown = normed_step(inputs, layer, layers, weights, lane_rows)
    if hub_old is not None:
        grown = grown + hub_old.astype(F32)
    return grown.astype(BF16)


def hout_kernel(plan, layer, layers, order, turned, rel_rows, lane_rows, weights, total_in, hub_sum, *refs):
    block = turned.shape[1]
    if layer == 1:
        total, hub_new = refs
        hub_old = None
    else:
        old, total, hub_new = refs
        hub_old = old[...]
    hub_new[...] = update_hubs(hub_sum[...], hub_old, layer - 1, layers, weights, lane_rows)
    for key in range(plan.keys[HOUT]):
        place = slice(key * block, (key + 1) * block)
        total[place, :] = total_in[place, :] + key_product(
            plan, layer, ((HOUT, hub_new),), key, order, turned, rel_rows
        )
    add_rest(plan, layer, HOUT, hub_new, order, turned, rel_rows, total)


def score_rows(values, width, layers, weights, lane_rows):
    lanes = values.shape[1]
    row = lax.broadcasted_iota(jnp.int32, (8, lanes), 0)
    column = lax.broadcasted_iota(jnp.int32, (8, lanes), 1)
    picks = jnp.where(lax.div(column, width) == row, lane_rows[2:3, :], 0.0)
    features = jnp.dot(values, weights[2 * layers], preferred_element_type=F32) + lane_rows[1:2, :]
    features = jnp.maximum(features, 0.0)
    high = features.astype(BF16)
    low = (features - high.astype(F32)).astype(BF16)
    pick_high = picks.astype(BF16)
    pick_low = (picks - pick_high.astype(F32)).astype(BF16)
    return contract_last(pick_high, high) + contract_last(pick_high, low) + contract_last(pick_low, high)


def close_kernel(plan, layer, layers, width, order, turned, rel_rows, lane_rows, lane_heads, weights, total_in, own, *refs):
    last = layer == layers - 1
    count = own.shape[0]
    block = turned.shape[1]
    first = lax.axis_index("ent") * count
    left, right, out, total = refs
    total[...] = total_in[...]
    add_rest(plan, layer, LEFT, left, order, turned, rel_rows, total)
    add_rest(plan, layer, RIGHT, right, order, turned, rel_rows, total)
    lane_q = lane_rows[0:1, :]
    for key in range(plan.keys[LEFT]):
        place = slice(key * block, (key + 1) * block)
        sums = total[place, :] + key_product(
            plan, layer, ((LEFT, left), (RIGHT, right)), key, order, turned, rel_rows
        )
        hits = hit_lanes(block, first + key * block, lane_heads[0:1, :], lane_q)
        inputs = (sums * lane_q + hits).astype(BF16)
        grown = normed_step(inputs, layer, layers, weights, lane_rows)
        new = (grown + own[place, :].astype(F32)).astype(BF16)
        if last:
            out[:, place] = score_rows(new, width, layers, weights, lane_rows)[: out.shape[0]]
        else:
            out[place, :] = new


def hub_kernel(layers, width, lane_rows, weights, hub_sum, hub_old, out):
    mine = out.shape[1]
    place = pl.ds(pl.multiple_of(lax.axis_index("ent") * mine, mine), mine)
    new = update_hubs(hub_sum[place, :], hub_old[place, :], layers - 1, layers, weights, lane_rows)
    out[...] = score_rows(new, width, layers, weights, lane_rows)[: out.shape[0]]


def body(
    ent_feat, query_head, query_rel, query_table, rel_table, layer_weight, layer_bias, norm_gain,
    norm_shift, reg_blocks, reg_rel, reg_mask, hin_blocks, hin_rel, hin_mask, hout_blocks,
    hout_rel, hout_mask, read_weight, read_bias, read_out,
):
    ends = lax.axis_size("ent")
    layers = rel_table.shape[0]
    q_local = query_head.shape[0] // lax.axis_size("qry")
    width, ent_local = ent_feat.shape
    block = reg_mask.shape[1]
    blocks = ent_local // block
    hubs = HUB_DEV * ends
    lanes = q_local * width
    counts = [reg_mask.shape[0], hin_mask.shape[0], hout_mask.shape[0]]
    tiles = sum(counts)
    plan = Plan(counts, blocks, hubs // block)
    padded = tiles + 8
    queries = query_head.shape[0]

    given = (
        reg_blocks.T, hin_blocks.T, hout_blocks.T, query_head,
        query_rel[None, :], reg_rel[None, :], hin_rel[None, :], hout_rel[None, :],
        query_table.T, jnp.swapaxes(rel_table, 1, 2), read_weight.T, read_bias[None, :],
        read_out[None, :], layer_weight, layer_bias, norm_gain, norm_shift,
        reg_mask, hin_mask, hout_mask,
    )
    outs = (
        ((tiles, block, block), BF16), ((layers, padded, lanes), F32),
        ((8 * ((3 + 3 * layers + 7) // 8), lanes), F32), ((8, lanes), jnp.int32),
        ((2 * layers + 2, lanes, lanes), BF16), ((plan.size,), jnp.int32),
    )
    stack_rows = queries + 8 * ((1 + 3 * layers + 7) // 8)
    turned, rel_rows, lane_rows, lane_heads, weights, order = pl.pallas_call(
        functools.partial(prep_kernel, plan, blocks, layers),
        in_specs=[pl.BlockSpec(memory_space=pltpu.HBM)] * len(given),
        out_specs=[VMEM] * 5 + [SMEM],
        out_shape=[jax.ShapeDtypeStruct(*o) for o in outs],
        scratch_shapes=[
            (pltpu.SMEM if i < 4 else pltpu.VMEM)(a.shape, a.dtype) for i, a in enumerate(given)
        ]
        + [
            pltpu.VMEM((stack_rows, width), F32),
            pltpu.VMEM((queries, width), F32),
            pltpu.SMEM((sum(plan.keys),), jnp.int32),
            pltpu.SMEM((8,), jnp.int32),
            pltpu.SemaphoreType.DMA((len(given),)),
        ],
        cost_estimate=pl.CostEstimate(
            flops=0, bytes_accessed=tiles * block * block * 6, transcendentals=0
        ),
        compiler_params=pltpu.CompilerParams(vmem_limit_bytes=24 << 20),
        name="prep",
    )(*(pltpu.with_memory_space_constraint(a, pltpu.HBM) for a in given))

    def shifts(cells):
        left = lax.ppermute(cells, "ent", [(i, i + 1) for i in range(ends - 1)])
        right = lax.ppermute(cells, "ent", [(i + 1, i) for i in range(ends - 1)])
        return left, right

    def exchanged(part, strides):
        for stride in strides:
            got = lax.ppermute(part, "ent", [(i, i ^ stride) for i in range(ends)])
            part = part + got
        return part

    far = [1 << i for i in range(1, ends.bit_length() - 1)]

    def call(kernel, operands, outs, scratch=(), tile_count=0, smem=1):
        return pl.pallas_call(
            kernel,
            in_specs=[SMEM] * smem + [VMEM] * (len(operands) - smem),
            out_specs=[VMEM] * len(outs),
            out_shape=outs,
            scratch_shapes=list(scratch),
            cost_estimate=pl.CostEstimate(
                flops=2 * tile_count * block * block * lanes,
                bytes_accessed=4 * tile_count * block * block,
                transcendentals=0,
            ),
            compiler_params=pltpu.CompilerParams(vmem_limit_bytes=16 << 20),
        )(*operands)

    state_shape = jax.ShapeDtypeStruct((ent_local, lanes), BF16)
    total_shape = jax.ShapeDtypeStruct((ent_local, lanes), F32)
    part_shape = jax.ShapeDtypeStruct((hubs, lanes), F32)
    hub_shape = jax.ShapeDtypeStruct((hubs, lanes), BF16)
    score_shape = jax.ShapeDtypeStruct((q_local, ent_local), F32)
    total_scratch = pltpu.VMEM((ent_local, lanes), F32)
    state_scratch = pltpu.VMEM((ent_local, lanes), BF16)
    tables = (order, turned, rel_rows)

    left, right = shifts(ent_feat)
    states, total, part = call(
        functools.partial(own_kernel, plan, 0),
        tables + (ent_feat, lane_rows, lane_heads),
        (state_shape, total_shape, part_shape), (), tiles // 2,
    )
    part, left, right = lax.optimization_barrier((part, left, right))
    part = exchanged(part, [1])
    left, right = call(
        functools.partial(side_kernel, block),
        (left, right, lane_rows, lane_heads), (state_shape, state_shape), (), tiles // 8, smem=0,
    )
    part, left, right = lax.optimization_barrier((part, left, right))
    part = exchanged(part, far[:1])

    def close(layer, total, states, left, right):
        last = layer == layers - 1
        (new,) = call(
            functools.partial(close_kernel, plan, layer, layers, width),
            tables + (lane_rows, lane_heads, weights, total, states, left, right),
            (score_shape if last else state_shape,), (total_scratch,), tiles // 2,
        )
        return new

    states = close(0, total, states, left, right)
    hub_old = None
    for layer in range(1, layers):
        last = layer == layers - 1
        states, part = lax.optimization_barrier((states, part))
        left, right = shifts(states)
        hub_sum = exchanged(part, far[1:]) if layer == 1 else part
        total, part = call(
            functools.partial(own_kernel, plan, layer),
            tables + (states,), (total_shape, part_shape), (), tiles // 2,
        )
        old = () if layer == 1 else (hub_old,)
        total, hub_old = call(
            functools.partial(hout_kernel, plan, layer, layers),
            tables + (lane_rows, weights, total, hub_sum) + old, (total_shape, hub_shape), (), tiles // 4,
        )
        part, total = lax.optimization_barrier((part, total))
        part = exchanged(part, far + [1])
        states = close(layer, total, states, left, right)
    hub_sum = part
    (hub_scores,) = call(
        functools.partial(hub_kernel, layers, width),
        (lane_rows, weights, hub_sum, hub_old), (jax.ShapeDtypeStruct((q_local, HUB_DEV), F32),), smem=0,
    )
    scores = lax.all_to_all(states, "qry", split_axis=1, concat_axis=0, tiled=True)
    return scores, hub_scores


def solution(mesh):
    return jax.shard_map(
        body,
        mesh=mesh,
        in_specs=(
            P(None, "ent"), P(), P(), P(), P(), P(), P(), P(), P(),
            P("ent", None), P("ent"), P("ent", None, None),
            P("ent", None), P("ent"), P("ent", None, None),
            P("ent", None), P("ent"), P("ent", None, None),
            P(), P(), P(),
        ),
        out_specs=(P(None, ("ent", "qry")), P("qry", "ent")),
        check_vma=False,
    )
```

time: 139 us -> 111 us (0.80)
  local copies, waits for them, and re-layouts: 18 us -> 0.62 us
  starting transfers between devices: 35.8 us -> 28.1 us
  Pallas kernels: 45.8 us -> 40.7 us
  waiting for transfers between devices: 38 us -> 40.3 us
    unnamed x42 -> x2, local copies, waits for them, and re-layouts: 17.3 us -> 0.01 us
    ppermute x9, starting transfers between devices: 20.2 us -> 10.1 us  [exchanged(): got = lax.ppermute(part, 'ent', [(i, i ^ stride) for i in range(ends)])]
    pallas_call x1, Pallas kernels: 14.1 us -> 8.95 us  [body(): pl.pallas_call(functools.partial(prep_kernel, plan, blocks, layers), in_s...]
    ppermute x3, starting transfers between devices: 8.45 us -> 10.9 us  [shifts(): left = lax.ppermute(cells, 'ent', [(i, i + 1) for i in range(ends - 1)])]
    ppermute x9, waiting for transfers between devices: 35.5 us -> 37.7 us  [exchanged(): got = lax.ppermute(part, 'ent', [(i, i ^ stride) for i in range(ends)])]
    pallas_call x9 -> x10, Pallas kernels: 31.7 us -> 31.8 us  [call(): pl.pallas_call(kernel, in_specs=[SMEM] * smem + [VMEM] * (len(operands) -...]
  transfers between devices with their start and end apart: 16 -> 16, of which waited for: 7 -> 7; matrix products, arithmetic and copies ran while one was open for 0% -> 0% of each run, Pallas kernels for 28% -> 32%
where the time goes in v3:
time: 111 us
  Pallas kernels  40.7 us (37%)
  waiting for transfers between devices  40.3 us (36%)
  starting transfers between devices  28.1 us (25%)
    ppermute x9, waiting for transfers between devices, exchanged(): got = lax.ppermute(part, 'ent', [(i, i ^ stride) for i in range(ends)])  37.7 us
    pallas_call x10, Pallas kernels, call(): pl.pallas_call(kernel, in_specs=[SMEM] * smem + [VMEM] * (len(operands) -...  31.8 us
    ppermute x3, starting transfers between devices, shifts(): left = lax.ppermute(cells, 'ent', [(i, i + 1) for i in range(ends - 1)])  10.9 us
    ppermute x9, starting transfers between devices, exchanged(): got = lax.ppermute(part, 'ent', [(i, i ^ stride) for i in range(ends)])  10.1 us
    pallas_call x1, Pallas kernels, body(): pl.pallas_call(functools.partial(prep_kernel, plan, blocks, layers), in_s...  8.95 us
    ppermute x3, starting transfers between devices, shifts(): right = lax.ppermute(cells, 'ent', [(i + 1, i) for i in range(ends - 1)])  3.88 us
    all_to_all x1, starting transfers between devices, body(): lax.all_to_all(states, 'qry', split_axis=1, concat_axis=0, tiled=True)  3.25 us
    all_to_all x1, waiting for transfers between devices, body(): lax.all_to_all(states, 'qry', split_axis=1, concat_axis=0, tiled=True)  2.65 us
  transfers between devices with their start and end apart: 16, of which 7 were waited for; matrix products, arithmetic and copies ran while one was open for 0% of the time, Pallas kernels for 32%

profile of v3, /device:TPU:0, one launch (start us, length us, event | category | flops | bytes accessed | tf_op | source)
XLA Modules:
  0.0 110.9 jit_solution(18259329832677876852)
XLA Ops:
  0.6 4.9 %collective-permute-start = (bf16[64,1024]{1,0:T(8,128)(2,1)}, bf16[64,1024]{1,0:T(8,128)(2,1)S(1)}, u32[]{:S(2)}, u32[]{:S(2)}) collective-permute-start(bf16[64,1024]{1,0:T(8,128)(2,1)} %refs_0_.1), channel_id=1, source_target_pairs={{0,4},{4,8},{8,12},{12,16},{16,20},{20,24},{24,28},{1,5},{5,9},{9,... | collective-permute-start | bytes 393224 | tf_op jit(solution)/shard_map/ppermute | solution.py:425
  6.8 9.0 %prep.1 = (bf16[128,128,128]{2,1,0:T(8,128)(2,1)S(1)}, f32[3,136,256]{2,1,0:T(8,128)S(1)}, f32[16,256]{1,0:T(8,128)S(1)}, s32[8,256]{1,0:T(8,128)S(1)}, bf16[8,2...) custom-call(s32[2,80]{1,0:T(2,128)} %bitcast.18, s32[2,24]{1,0:T(2,128)} %bitcast.19, s32[2,24]{1,0:T(2,128)} %bitcast.20, ...), custom_call_target="tpu_custom_call" | custom-call | bytes 12582912 | tf_op jit(solution)/shard_map/prep/pallas_call | solution.py:402
  15.8 3.7 %shard_map.212 = (bf16[1024,256]{1,0:T(8,128)(2,1)S(1)}, f32[1024,256]{1,0:T(8,128)S(1)}, f32[128,256]{1,0:T(8,128)S(1)}) custom-call(s32[520]{0:T(1024)S(1)} %get-tuple-element.35.order, bf16[128,128,128]{2,1,0:T(8,128)(2,1)S(1)} %get-tuple-element.36.turned, f32[3,136,256]{2,1,0:T(8,128)S(1)} %get-tuple-element.37.rel_rows, bf16[64,1024]{1,0:T(8,128)(2,1)S(1)} %copy-done, ...), custom_call_target="tpu_custom_call" | custom-call | flops 536870912 | bytes 4194304 | tf_op jit(solution)/shard_map/pallas_call | solution.py:438
  21.2 3.4 %collective-permute-done.2 = f32[128,256]{1,0:T(8,128)S(1)} collective-permute-done((f32[128,256]{1,0:T(8,128)S(1)}, f32[128,256]{1,0:T(8,128)S(1)}, u32[]{:S(2)}, u32[]{:S(2)}) %collective-permute-start.2) | collective-permute-done | bytes 131104 | tf_op jit(solution)/shard_map/ppermute | solution.py:431
  24.6 2.1 %collective-permute-start.3 = (f32[128,256]{1,0:T(8,128)S(1)}, f32[128,256]{1,0:T(8,128)S(1)}, u32[]{:S(2)}, u32[]{:S(2)}) collective-permute-start(f32[128,256]{1,0:T(8,128)S(1)} %add.27), channel_id=1, source_target_pairs={{0,8},{4,12},{8,0},{12,4},{16,24},{20,28},{24,16},{28,20},{1,9},{5... | collective-permute-start | bytes 393224 | tf_op jit(solution)/shard_map/ppermute | solution.py:431
  26.7 5.0 %shard_map.214.refs_0_.own = bf16[1024,256]{1,0:T(8,128)(2,1)S(1)} custom-call(s32[520]{0:T(1024)S(1)} %get-tuple-element.35.order, bf16[128,128,128]{2,1,0:T(8,128)(2,1)S(1)} %get-tuple-element.36.turned, f32[3,136,256]{2,1,0:T(8,128)S(1)} %get-tuple-element.37.rel_rows, f32[16,256]{1,0:T(8,128)S(1)} %get-tuple-element.38.refs_1_.lane_rows, ...), custom_call_target="tpu_custom_call" | custom-call | flops 536870912 | bytes 4194304 | tf_op jit(solution)/shard_map/pallas_call | solution.py:438
  31.7 3.7 %collective-permute-start.4 = (f32[128,256]{1,0:T(8,128)S(1)}, f32[128,256]{1,0:T(8,128)S(1)}, u32[]{:S(2)}, u32[]{:S(2)}) collective-permute-start(f32[128,256]{1,0:T(8,128)S(1)} %add.28), channel_id=1, source_target_pairs={{0,16},{4,20},{8,24},{12,28},{16,0},{20,4},{24,8},{28,12},{1,17},{... | collective-permute-start | bytes 393224 | tf_op jit(solution)/shard_map/ppermute | solution.py:431
  35.4 4.1 %collective-permute-start.5 = (bf16[1024,256]{1,0:T(8,128)(2,1)S(1)}, bf16[1024,256]{1,0:T(8,128)(2,1)S(1)}, u32[]{:S(2)}, u32[]{:S(2)}) collective-permute-start(bf16[1024,256]{1,0:T(8,128)(2,1)S(1)} %shard_map.214.refs_0_.own), channel_id=1, source_target_pairs={{0,4},{4,8},{8,12},{12,16},{16,20},{20,24},{24,28},{1,5},{5,9},{9,... | collective-permute-start | bytes 1572872 | tf_op jit(solution)/shard_map/ppermute | solution.py:425
  39.5 1.3 %collective-permute-start.6 = (bf16[1024,256]{1,0:T(8,128)(2,1)S(1)}, bf16[1024,256]{1,0:T(8,128)(2,1)S(1)}, u32[]{:S(2)}, u32[]{:S(2)}) collective-permute-start(bf16[1024,256]{1,0:T(8,128)(2,1)S(1)} %shard_map.214.refs_0_.own), channel_id=1, source_target_pairs={{4,0},{8,4},{12,8},{16,12},{20,16},{24,20},{28,24},{5,1},{9,5},{13... | collective-permute-start | bytes 1572872 | tf_op jit(solution)/shard_map/ppermute | solution.py:426
  40.8 3.2 %shard_map.215 = (f32[1024,256]{1,0:T(8,128)S(1)}, f32[128,256]{1,0:T(8,128)S(1)}) custom-call(s32[520]{0:T(1024)S(1)} %get-tuple-element.35.order, bf16[128,128,128]{2,1,0:T(8,128)(2,1)S(1)} %get-tuple-element.36.turned, f32[3,136,256]{2,1,0:T(8,128)S(1)} %get-tuple-element.37.rel_rows, bf16[1024,256]{1,0:T(8,128)(2,1)S(1)} %shard_map.214.refs_0_.own), custom_call_target="tpu_custom_call" | custom-call | flops 536870912 | bytes 4194304 | tf_op jit(solution)/shard_map/pallas_call | solution.py:438
  44.1 1.7 %shard_map.216 = (f32[1024,256]{1,0:T(8,128)S(1)}, bf16[128,256]{1,0:T(8,128)(2,1)S(1)}) custom-call(s32[520]{0:T(1024)S(1)} %get-tuple-element.35.order, bf16[128,128,128]{2,1,0:T(8,128)(2,1)S(1)} %get-tuple-element.36.turned, f32[3,136,256]{2,1,0:T(8,128)S(1)} %get-tuple-element.37.rel_rows, f32[16,256]{1,0:T(8,128)S(1)} %get-tuple-element.38.refs_1_.lane_rows, ...), custom_call_target="tpu_custom_call" | custom-call | flops 268435456 | bytes 2097152 | tf_op jit(solution)/shard_map/pallas_call | solution.py:438
  46.3 8.8 %collective-permute-done.7 = f32[128,256]{1,0:T(8,128)S(1)} collective-permute-done((f32[128,256]{1,0:T(8,128)S(1)}, f32[128,256]{1,0:T(8,128)S(1)}, u32[]{:S(2)}, u32[]{:S(2)}) %collective-permute-start.7) | collective-permute-done | bytes 131104 | tf_op jit(solution)/shard_map/ppermute | solution.py:431
  55.9 5.5 %collective-permute-done.8 = f32[128,256]{1,0:T(8,128)S(1)} collective-permute-done((f32[128,256]{1,0:T(8,128)S(1)}, f32[128,256]{1,0:T(8,128)S(1)}, u32[]{:S(2)}, u32[]{:S(2)}) %collective-permute-start.8) | collective-permute-done | bytes 131104 | tf_op jit(solution)/shard_map/ppermute | solution.py:431
  61.5 5.0 %collective-permute-done.9 = f32[128,256]{1,0:T(8,128)S(1)} collective-permute-done((f32[128,256]{1,0:T(8,128)S(1)}, f32[128,256]{1,0:T(8,128)S(1)}, u32[]{:S(2)}, u32[]{:S(2)}) %collective-permute-start.9) | collective-permute-done | bytes 131104 | tf_op jit(solution)/shard_map/ppermute | solution.py:431
  66.5 5.1 %shard_map.217.refs_0_.own = bf16[1024,256]{1,0:T(8,128)(2,1)S(1)} custom-call(s32[520]{0:T(1024)S(1)} %get-tuple-element.35.order, bf16[128,128,128]{2,1,0:T(8,128)(2,1)S(1)} %get-tuple-element.36.turned, f32[3,136,256]{2,1,0:T(8,128)S(1)} %get-tuple-element.37.rel_rows, f32[16,256]{1,0:T(8,128)S(1)} %get-tuple-element.38.refs_1_.lane_rows, ...), custom_call_target="tpu_custom_call" | custom-call | flops 536870912 | bytes 4194304 | tf_op jit(solution)/shard_map/pallas_call | solution.py:438
  71.7 1.9 %collective-permute-start.10 = (bf16[1024,256]{1,0:T(8,128)(2,1)S(1)}, bf16[1024,256]{1,0:T(8,128)(2,1)S(1)}, u32[]{:S(2)}, u32[]{:S(2)}) collective-permute-start(bf16[1024,256]{1,0:T(8,128)(2,1)S(1)} %shard_map.217.refs_0_.own), channel_id=1, source_target_pairs={{0,4},{4,8},{8,12},{12,16},{16,20},{20,24},{24,28},{1,5},{5,9},{9,... | collective-permute-start | bytes 1572872 | tf_op jit(solution)/shard_map/ppermute | solution.py:425
  74.9 3.2 %shard_map.218 = (f32[1024,256]{1,0:T(8,128)S(1)}, f32[128,256]{1,0:T(8,128)S(1)}) custom-call(s32[520]{0:T(1024)S(1)} %get-tuple-element.35.order, bf16[128,128,128]{2,1,0:T(8,128)(2,1)S(1)} %get-tuple-element.36.turned, f32[3,136,256]{2,1,0:T(8,128)S(1)} %get-tuple-element.37.rel_rows, bf16[1024,256]{1,0:T(8,128)(2,1)S(1)} %shard_map.217.refs_0_.own), custom_call_target="tpu_custom_call" | custom-call | flops 536870912 | bytes 4194304 | tf_op jit(solution)/shard_map/pallas_call | solution.py:438
  78.1 1.6 %shard_map.219 = (f32[1024,256]{1,0:T(8,128)S(1)}, bf16[128,256]{1,0:T(8,128)(2,1)S(1)}) custom-call(s32[520]{0:T(1024)S(1)} %get-tuple-element.35.order, bf16[128,128,128]{2,1,0:T(8,128)(2,1)S(1)} %get-tuple-element.36.turned, f32[3,136,256]{2,1,0:T(8,128)S(1)} %get-tuple-element.37.rel_rows, f32[16,256]{1,0:T(8,128)S(1)} %get-tuple-element.38.refs_1_.lane_rows, ...), custom_call_target="tpu_custom_call" | custom-call | flops 268435456 | bytes 2097152 | tf_op jit(solution)/shard_map/pallas_call | solution.py:438
  79.8 1.5 %collective-permute-start.12 = (f32[128,256]{1,0:T(8,128)S(1)}, f32[128,256]{1,0:T(8,128)S(1)}, u32[]{:S(2)}, u32[]{:S(2)}) collective-permute-start(f32[128,256]{1,0:T(8,128)S(1)} %get-tuple-element.66), channel_id=1, source_target_pairs={{0,8},{4,12},{8,0},{12,4},{16,24},{20,28},{24,16},{28,20},{1,9},{5... | collective-permute-start | bytes 393224 | tf_op jit(solution)/shard_map/ppermute | solution.py:431
  81.3 8.8 %collective-permute-done.12 = f32[128,256]{1,0:T(8,128)S(1)} collective-permute-done((f32[128,256]{1,0:T(8,128)S(1)}, f32[128,256]{1,0:T(8,128)S(1)}, u32[]{:S(2)}, u32[]{:S(2)}) %collective-permute-start.12) | collective-permute-done | bytes 131104 | tf_op jit(solution)/shard_map/ppermute | solution.py:431
  90.2 6.2 %collective-permute-done.13 = f32[128,256]{1,0:T(8,128)S(1)} collective-permute-done((f32[128,256]{1,0:T(8,128)S(1)}, f32[128,256]{1,0:T(8,128)S(1)}, u32[]{:S(2)}, u32[]{:S(2)}) %collective-permute-start.13) | collective-permute-done | bytes 131104 | tf_op jit(solution)/shard_map/ppermute | solution.py:431
  96.6 6.6 %shard_map.220 = f32[4,1024]{1,0:T(4,128)} custom-call(s32[520]{0:T(1024)S(1)} %get-tuple-element.35.order, bf16[128,128,128]{2,1,0:T(8,128)(2,1)S(1)} %get-tuple-element.36.turned, f32[3,136,256]{2,1,0:T(8,128)S(1)} %get-tuple-element.37.rel_rows, f32[16,256]{1,0:T(8,128)S(1)} %get-tuple-element.38.refs_1_.lane_rows, ...), custom_call_target="tpu_custom_call" | custom-call | flops 536870912 | bytes 4194304 | tf_op jit(solution)/shard_map/pallas_call | solution.py:438
  103.2 3.3 %all-to-all-start = ((f32[4,4,256]{2,0,1:T(4,128)}), f32[4,4,256]{2,0,1:T(4,128)S(1)}, u32[]{:S(2)}, u32[]{:S(2)}) async-start(f32[4,4,256]{2,0,1:T(4,128)} %bitcast.12), calls=%async_computation | async-start | bytes 32768 | tf_op jit(solution)/shard_map/all_to_all | solution.py:509
  107.6 2.6 %all-to-all-done = f32[4,4,256]{2,0,1:T(4,128)S(1)} async-done(((f32[4,4,256]{2,0,1:T(4,128)}), f32[4,4,256]{2,0,1:T(4,128)S(1)}, u32[]{:S(2)}, u32[]{:S(2)}) %all-to-all-start) | async-done | bytes 16416 | tf_op jit(solution)/shard_map/all_to_all | solution.py:509
  (31 shorter events, 7.8 us)
Async XLA Ops:
  0.6 18.9 %collective-permute-start = (bf16[64,1024]{1,0:T(8,128)(2,1)}, bf16[64,1024]{1,0:T(8,128)(2,1)S(1)}, u32[]{:S(2)}, u32[]{:S(2)}) collective-permute-start(bf16[64,1024]{1,0:T(8,128)(2,1)} %refs_0_.1), channel_id=1, source_target_pairs={{0,4},{4,8},{8,12},{12,16},{16,20},{20,24},{24,28},{1,5},{5,9},{9,... | collective-permute-start | bytes 393224 | tf_op jit(solution)/shard_map/ppermute | solution.py:425
  5.5 14.0 %collective-permute-start.1 = (bf16[64,1024]{1,0:T(8,128)(2,1)}, bf16[64,1024]{1,0:T(8,128)(2,1)S(1)}, u32[]{:S(2)}, u32[]{:S(2)}) collective-permute-start(bf16[64,1024]{1,0:T(8,128)(2,1)} %refs_0_.1), channel_id=1, source_target_pairs={{4,0},{8,4},{12,8},{16,12},{20,16},{24,20},{28,24},{5,1},{9,5},{13... | collective-permute-start | bytes 393224 | tf_op jit(solution)/shard_map/ppermute | solution.py:426
  6.8 9.0 %copy-start = (bf16[64,1024]{1,0:T(8,128)(2,1)S(1)}, bf16[64,1024]{1,0:T(8,128)(2,1)}, u32[]{:S(2)}) copy-start(bf16[64,1024]{1,0:T(8,128)(2,1)} %refs_0_.1) | copy-start | bytes 393220
  19.5 5.0 %collective-permute-start.2 = (f32[128,256]{1,0:T(8,128)S(1)}, f32[128,256]{1,0:T(8,128)S(1)}, u32[]{:S(2)}, u32[]{:S(2)}) collective-permute-start(f32[128,256]{1,0:T(8,128)S(1)} %get-tuple-element.44), channel_id=1, source_target_pairs={{0,4},{4,0},{8,12},{12,8},{16,20},{20,16},{24,28},{28,24},{1,5},{5... | collective-permute-start | bytes 393224 | tf_op jit(solution)/shard_map/ppermute | solution.py:431
  24.6 7.1 %collective-permute-start.3 = (f32[128,256]{1,0:T(8,128)S(1)}, f32[128,256]{1,0:T(8,128)S(1)}, u32[]{:S(2)}, u32[]{:S(2)}) collective-permute-start(f32[128,256]{1,0:T(8,128)S(1)} %add.27), channel_id=1, source_target_pairs={{0,8},{4,12},{8,0},{12,4},{16,24},{20,28},{24,16},{28,20},{1,9},{5... | collective-permute-start | bytes 393224 | tf_op jit(solution)/shard_map/ppermute | solution.py:431
  31.7 12.3 %collective-permute-start.4 = (f32[128,256]{1,0:T(8,128)S(1)}, f32[128,256]{1,0:T(8,128)S(1)}, u32[]{:S(2)}, u32[]{:S(2)}) collective-permute-start(f32[128,256]{1,0:T(8,128)S(1)} %add.28), channel_id=1, source_target_pairs={{0,16},{4,20},{8,24},{12,28},{16,0},{20,4},{24,8},{28,12},{1,17},{... | collective-permute-start | bytes 393224 | tf_op jit(solution)/shard_map/ppermute | solution.py:431
  35.4 31.1 %collective-permute-start.5 = (bf16[1024,256]{1,0:T(8,128)(2,1)S(1)}, bf16[1024,256]{1,0:T(8,128)(2,1)S(1)}, u32[]{:S(2)}, u32[]{:S(2)}) collective-permute-start(bf16[1024,256]{1,0:T(8,128)(2,1)S(1)} %shard_map.214.refs_0_.own), channel_id=1, source_target_pairs={{0,4},{4,8},{8,12},{12,16},{16,20},{20,24},{24,28},{1,5},{5,9},{9,... | collective-permute-start | bytes 1572872 | tf_op jit(solution)/shard_map/ppermute | solution.py:425
  39.5 27.0 %collective-permute-start.6 = (bf16[1024,256]{1,0:T(8,128)(2,1)S(1)}, bf16[1024,256]{1,0:T(8,128)(2,1)S(1)}, u32[]{:S(2)}, u32[]{:S(2)}) collective-permute-start(bf16[1024,256]{1,0:T(8,128)(2,1)S(1)} %shard_map.214.refs_0_.own), channel_id=1, source_target_pairs={{4,0},{8,4},{12,8},{16,12},{20,16},{24,20},{28,24},{5,1},{9,5},{13... | collective-permute-start | bytes 1572872 | tf_op jit(solution)/shard_map/ppermute | solution.py:426
  45.8 9.4 %collective-permute-start.7 = (f32[128,256]{1,0:T(8,128)S(1)}, f32[128,256]{1,0:T(8,128)S(1)}, u32[]{:S(2)}, u32[]{:S(2)}) collective-permute-start(f32[128,256]{1,0:T(8,128)S(1)} %get-tuple-element.58), channel_id=1, source_target_pairs={{0,8},{4,12},{8,0},{12,4},{16,24},{20,28},{24,16},{28,20},{1,9},{5... | collective-permute-start | bytes 393224 | tf_op jit(solution)/shard_map/ppermute | solution.py:431
  55.1 6.3 %collective-permute-start.8 = (f32[128,256]{1,0:T(8,128)S(1)}, f32[128,256]{1,0:T(8,128)S(1)}, u32[]{:S(2)}, u32[]{:S(2)}) collective-permute-start(f32[128,256]{1,0:T(8,128)S(1)} %add.30), channel_id=1, source_target_pairs={{0,16},{4,20},{8,24},{12,28},{16,0},{20,4},{24,8},{28,12},{1,17},{... | collective-permute-start | bytes 393224 | tf_op jit(solution)/shard_map/ppermute | solution.py:431
  61.5 5.0 %collective-permute-start.9 = (f32[128,256]{1,0:T(8,128)S(1)}, f32[128,256]{1,0:T(8,128)S(1)}, u32[]{:S(2)}, u32[]{:S(2)}) collective-permute-start(f32[128,256]{1,0:T(8,128)S(1)} %add.31), channel_id=1, source_target_pairs={{0,4},{4,0},{8,12},{12,8},{16,20},{20,16},{24,28},{28,24},{1,5},{5... | collective-permute-start | bytes 393224 | tf_op jit(solution)/shard_map/ppermute | solution.py:431
  71.7 24.9 %collective-permute-start.10 = (bf16[1024,256]{1,0:T(8,128)(2,1)S(1)}, bf16[1024,256]{1,0:T(8,128)(2,1)S(1)}, u32[]{:S(2)}, u32[]{:S(2)}) collective-permute-start(bf16[1024,256]{1,0:T(8,128)(2,1)S(1)} %shard_map.217.refs_0_.own), channel_id=1, source_target_pairs={{0,4},{4,8},{8,12},{12,16},{16,20},{20,24},{24,28},{1,5},{5,9},{9,... | collective-permute-start | bytes 1572872 | tf_op jit(solution)/shard_map/ppermute | solution.py:425
  73.6 22.9 %collective-permute-start.11 = (bf16[1024,256]{1,0:T(8,128)(2,1)S(1)}, bf16[1024,256]{1,0:T(8,128)(2,1)S(1)}, u32[]{:S(2)}, u32[]{:S(2)}) collective-permute-start(bf16[1024,256]{1,0:T(8,128)(2,1)S(1)} %shard_map.217.refs_0_.own), channel_id=1, source_target_pairs={{4,0},{8,4},{12,8},{16,12},{20,16},{24,20},{28,24},{5,1},{9,5},{13... | collective-permute-start | bytes 1572872 | tf_op jit(solution)/shard_map/ppermute | solution.py:426
  79.8 10.3 %collective-permute-start.12 = (f32[128,256]{1,0:T(8,128)S(1)}, f32[128,256]{1,0:T(8,128)S(1)}, u32[]{:S(2)}, u32[]{:S(2)}) collective-permute-start(f32[128,256]{1,0:T(8,128)S(1)} %get-tuple-element.66), channel_id=1, source_target_pairs={{0,8},{4,12},{8,0},{12,4},{16,24},{20,28},{24,16},{28,20},{1,9},{5... | collective-permute-start | bytes 393224 | tf_op jit(solution)/shard_map/ppermute | solution.py:431
  90.1 6.3 %collective-permute-start.13 = (f32[128,256]{1,0:T(8,128)S(1)}, f32[128,256]{1,0:T(8,128)S(1)}, u32[]{:S(2)}, u32[]{:S(2)}) collective-permute-start(f32[128,256]{1,0:T(8,128)S(1)} %add.33), channel_id=1, source_target_pairs={{0,16},{4,20},{8,24},{12,28},{16,0},{20,4},{24,8},{28,12},{1,17},{... | collective-permute-start | bytes 393224 | tf_op jit(solution)/shard_map/ppermute | solution.py:431
  96.5 10.0 %collective-permute-start.14 = (f32[128,256]{1,0:T(8,128)S(1)}, f32[128,256]{1,0:T(8,128)S(1)}, u32[]{:S(2)}, u32[]{:S(2)}) collective-permute-start(f32[128,256]{1,0:T(8,128)S(1)} %add.34), channel_id=1, source_target_pairs={{0,4},{4,0},{8,12},{12,8},{16,20},{20,16},{24,28},{28,24},{1,5},{5... | collective-permute-start | bytes 393224 | tf_op jit(solution)/shard_map/ppermute | solution.py:431
  103.2 7.1 %all-to-all-start = ((f32[4,4,256]{2,0,1:T(4,128)}), f32[4,4,256]{2,0,1:T(4,128)S(1)}, u32[]{:S(2)}, u32[]{:S(2)}) async-start(f32[4,4,256]{2,0,1:T(4,128)} %bitcast.12), calls=%async_computation | async-start | bytes 32768 | tf_op jit(solution)/shard_map/all_to_all | solution.py:509
